TPU v7x, 768 devices: a whole 4x8x12 slice. The times are simulated.
768 devices in a mesh: dp: 96 (over y, z), tensor: 8 (over x, core).
Axes of the slice: x: 4, y: 8, z: 12, core: 2. Of those that a mesh axis runs over, the one named last changes fastest.
Arguments:
- gradients: bfloat16 [96, 1344, 4096], P('dp', None, 'tensor'), may hold values from -12 to 12
- error_buffer: bfloat16 [96, 1344, 4096], P('dp', None, 'tensor'), may hold values from -6 to 6
- warm_basis: float32 [4096, 32], P('tensor'), may hold values from -6 to 6
Outputs:
- new_errors: bfloat16 [96, 1344, 4096], P('dp', None, 'tensor')
- new_basis: float32 [4096, 32], P('tensor')
All inputs are finite; a program needn't handle non-finite values.
Results may differ from a plain program's by a relative error of at most 0.001.
Values sent between devices are 32-bit elements; how exact they have to be, the bound alone decides.
A program may use at most 32 MiB of HBM per device.

v0:
```python
import jax
import jax.numpy as jnp
from jax import lax
from jax.sharding import PartitionSpec as P

REPLICAS = 8


def orthonormal(left_rows, gram_matrix):
    lower_factor = jnp.linalg.cholesky(gram_matrix)
    return lax.linalg.triangular_solve(
        lower_factor, left_rows, left_side=False, lower=True, transpose_a=True
    )


def on_device(gradients, error_buffer, warm_basis):
    highest = lax.Precision.HIGHEST
    dp_count = lax.axis_size("dp")
    split = dp_count // REPLICAS
    block_index = lax.axis_index("dp") % split
    block_rows = gradients.shape[1]
    rank_width = warm_basis.shape[1]
    merged = gradients[0].astype(jnp.float32) + error_buffer[0].astype(jnp.float32)
    left_partial = jnp.dot(
        merged, warm_basis, precision=highest, preferred_element_type=jnp.float32
    )
    offset = block_index * block_rows
    padded = lax.dynamic_update_slice_in_dim(
        jnp.zeros((split * block_rows, rank_width), jnp.float32), left_partial, offset, 0
    )
    left_factor = lax.psum(padded, ("dp", "tensor")) / REPLICAS
    gram_matrix = jnp.dot(
        left_factor.T, left_factor, precision=highest, preferred_element_type=jnp.float32
    )
    basis_left = orthonormal(left_factor, gram_matrix)
    basis_own = lax.dynamic_slice_in_dim(basis_left, offset, block_rows, 0)
    right_partial = lax.dot_general(
        merged,
        basis_own,
        (((0,), (0,)), ((), ())),
        precision=highest,
        preferred_element_type=jnp.float32,
    )
    new_basis = lax.psum(right_partial, "dp") / REPLICAS
    rebuilt = lax.dot_general(
        basis_own,
        new_basis,
        (((1,), (1,)), ((), ())),
        precision=highest,
        preferred_element_type=jnp.float32,
    )
    new_errors = (merged - rebuilt).astype(jnp.bfloat16)
    return (new_errors[None], new_basis)


def solution(mesh):
    placed = (P("dp", None, "tensor"), P("dp", None, "tensor"), P("tensor", None))
    return jax.shard_map(
        on_device,
        mesh=mesh,
        in_specs=placed,
        out_specs=(P("dp", None, "tensor"), P("tensor", None)),
        check_vma=False,
    )
```

profile of v0, /device:TPU:1, one launch (start us, length us, event | category | flops | bytes accessed | tf_op | source)
XLA Modules:
  0.0 745.5 jit_solution(5596786265300273155)
XLA Ops:
  7.2 0.0 copy-start
  7.2 0.0 all-reduce.3.cloned.1.call-start
  7.3 0.8 copy-done
  8.0 4.4 fusion.3
  12.5 0.1 broadcast_in_dim.8
  12.6 1.5 dynamic_update_slice.3
  14.1 0.0 copy-start.3
  14.1 1.3 copy-done.3
  15.4 0.0 all-reduce.3.cloned.1.call-update
  15.4 0.2 all-reduce.5.cloned.1.call-start
  15.6 486.9 %all-reduce.3.cloned.1.call-done = f32[16128,32]{0,1:T(8,128)} async-done(((f32[16128,32]{0,1:T(8,128)}), f32[16128,32]{0,1:T(8,128)}) %all-reduce.3.cloned.1.call-update) | async-done | bytes 2064400 | tf_op jit(solution)/shard_map/psum | solution.py:31
  502.6 4.1 fusion.8
  506.7 0.1 copy.5
  506.7 2.9 cholesky.16
  509.7 0.6 compare_reduce_fusion
  510.3 0.7 fusion.14
  511.0 2.4 custom-call.6
  513.4 0.0 copy-start.1
  513.4 0.0 copy-start.2
  513.4 3.7 fusion.6
  517.1 0.0 copy-start.4
  517.1 1.3 copy-done.4
  518.5 0.0 copy-done.1
  518.5 0.0 copy-done.2
  518.5 2.7 fusion.1
  521.1 0.0 all-reduce.5.cloned.1.call-update
  521.1 211.7 %all-reduce.5.cloned.1.call-done = f32[512,32]{0,1:T(8,128)} async-done(((f32[512,32]{0,1:T(8,128)}), f32[512,32]{0,1:T(8,128)}) %all-reduce.5.cloned.1.call-update) | async-done | bytes 65552 | tf_op jit(solution)/shard_map/psum | solution.py:44
  732.9 0.8 broadcast_multiply_fusion
  733.7 0.0 copy-start.5
  733.7 4.9 fusion.5
  738.6 0.0 copy-done.5
  (2 shorter events, 0.0 us)
Async XLA Ops:
  7.2 0.8 copy-start
  7.2 495.4 %all-reduce.3.cloned.1.call-start = ((), (), s32[]{:S(2)}) async-start(), calls=%async_computation | async-start | bytes 4128768 | tf_op jit(solution)/shard_map/psum | solution.py:31
  14.1 1.3 copy-start.3
  15.4 717.5 %all-reduce.5.cloned.1.call-start = ((), (), s32[]{:S(2)}) async-start(), calls=%async_computation.1 | async-start | bytes 131072 | tf_op jit(solution)/shard_map/psum | solution.py:44
  513.4 5.0 copy-start.1
  513.4 5.0 copy-start.2
  517.1 1.3 copy-start.4
  733.7 4.9 copy-start.5
Sparse Core Ops, SparseCore 0:
  15.5 486.9 all-reduce.2
  521.3 211.5 all-reduce.4
where the time goes:
time: 752 us; the launch traced here: 745 us
  waiting for transfers between devices  699 us (93%)
  matrix products  19.8 us (3%)
  between operations  14.1 us (2%)
  other arithmetic  7.53 us (1%)
    psum x1, waiting for transfers between devices, on_device(): left_factor = lax.psum(padded, ('dp', 'tensor')) / REPLICAS  487 us
    psum x1, waiting for transfers between devices, on_device(): new_basis = lax.psum(right_partial, 'dp') / REPLICAS  212 us
  transfers between devices with their start and end apart: 2, of which 2 were waited for; matrix products, arithmetic and copies ran while one was open for 0% of the time, Pallas kernels for 0%

commit v1 on v0

v1 whole, which is shorter than its diff:
```python
import jax
import jax.numpy as jnp
from jax import lax
from jax.experimental import pallas as pl
from jax.experimental.pallas import tpu as pltpu
from jax.sharding import PartitionSpec as P

MESH = pl.DeviceIdType.MESH
HIGHEST = lax.Precision.HIGHEST
F32 = jnp.float32
BF16 = jnp.bfloat16

NY = 8
NZ = 12
NT = 8
ROWS = 1344
COLS = 512
RANK = 32
GROUPS = 4
GROUP_ROWS = 384
HALF = 192
PIECE = GROUP_ROWS // NT
CHUNKS = 3
CHUNK = PIECE // CHUNKS
RCOLS = 256

ORDER8 = (4, 3, 5, 2, 6, 1, 7)
ORDER12 = (6, 5, 7, 4, 8, 3, 9, 2, 10, 1, 11)


def split2(x):
    hi = x.astype(BF16)
    return hi, (x - hi.astype(F32)).astype(BF16)


def split3(x):
    hi = x.astype(BF16)
    rest = x - hi.astype(F32)
    mid = rest.astype(BF16)
    return hi, mid, (rest - mid.astype(F32)).astype(BF16)


def row_bands(x, group):
    n = x.shape[1]
    parts = []
    if group:
        parts.append(jnp.zeros((RANK * group, n), x.dtype))
    parts.append(x)
    if group < GROUPS - 1:
        parts.append(jnp.zeros((RANK * (GROUPS - 1 - group), n), x.dtype))
    return jnp.concatenate(parts, axis=0)


def inverse_lower(gram):
    lane = lax.broadcasted_iota(jnp.int32, (RANK, 128), 1)
    row = lax.broadcasted_iota(jnp.int32, (RANK, 128), 0)
    a = jnp.where(lane < RANK, gram, jnp.where(lane == row + RANK, 1.0, 0.0))
    for k in range(RANK - 1):
        pivot = a[k : k + 1, :]
        factor = a[:, k : k + 1] * (1.0 / pivot[:, k : k + 1])
        factor = jnp.where(row[:, :1] > k, factor, 0.0)
        a = a - factor * pivot
    diagonal = jnp.sum(jnp.where(lane == row, a, 0.0), axis=1, keepdims=True)
    inv = a * lax.rsqrt(diagonal)
    inv = jnp.where((lane >= RANK) & (lane < 2 * RANK), inv, 0.0)
    inv = inv + pltpu.roll(inv, 2 * RANK, 1)
    return inv + pltpu.roll(inv, RANK, 1)


def comm_kernel(
    g_hbm, e_hbm, wt_ref, p_out, rt_out, l_out,
    gv, ev, part, xbuf, ybuf, pfull, rpart, rsbuf, zbuf, gbuf, rfull,
    load_sem, xs, xr, ys, yr, ps, pr, gs, gr, rs, rr, zs, zr, fs, fr,
):
    dp = lax.axis_index("dp")
    t = lax.axis_index("tensor")
    y = lax.div(dp, NZ)
    z = lax.rem(dp, NZ)

    def t_peer(k):
        return {"dp": dp, "tensor": lax.rem(t + k, NT)}

    def y_peer(k):
        return {"dp": lax.rem(y + k, NY) * NZ + z, "tensor": t}

    def z_peer(k):
        return {"dp": y * NZ + lax.rem(z + k, NZ), "tensor": t}

    def send(src, dst, ssem, rsem, peer):
        copy = pltpu.make_async_remote_copy(
            src_ref=src, dst_ref=dst, send_sem=ssem, recv_sem=rsem, device_id=peer, device_id_type=MESH
        )
        copy.start()
        return copy

    loads = []
    for j in range(GROUPS):
        rows = pl.ds(GROUP_ROWS * j, GROUP_ROWS if j < GROUPS - 1 else HALF)
        pair = [
            pltpu.make_async_copy(g_hbm.at[rows], gv.at[rows], load_sem.at[0, j]),
            pltpu.make_async_copy(e_hbm.at[rows], ev.at[rows], load_sem.at[1, j]),
        ]
        for copy in pair:
            copy.start()
        loads.append(pair)

    barrier = pltpu.get_barrier_semaphore()
    for k in ORDER12:
        pl.semaphore_signal(barrier, inc=1, device_id=z_peer(k), device_id_type=MESH)
    for k in ORDER8:
        pl.semaphore_signal(barrier, inc=1, device_id=y_peer(k), device_id_type=MESH)
        pl.semaphore_signal(barrier, inc=1, device_id=t_peer(k), device_id_type=MESH)

    w_hi, w_lo = split2(wt_ref[...] * (1.0 / NY))
    acc = [None, None]
    nt_dims = (((1,), (1,)), ((), ()))
    for j in range(GROUPS):
        weights = jnp.concatenate([row_bands(w_hi, j), row_bands(w_lo, j)], axis=0)
        for copy in loads[j]:
            copy.wait()
        for h in range(2 if j < GROUPS - 1 else 1):
            start = GROUP_ROWS * j + HALF * h
            for ref in (gv, ev):
                term = lax.dot_general(
                    ref[start : start + HALF, :], weights, nt_dims, preferred_element_type=F32
                )
                acc[h] = term if acc[h] is None else acc[h] + term
    for h in range(2):
        packed = acc[h][:, :128] + acc[h][:, 128:]
        for i in range(NT // 2):
            part[h * (NT // 2) + i] = packed[PIECE * i : PIECE * (i + 1)]

    pl.semaphore_wait(barrier, NZ + NY + NT - 3)

    sent = []
    got_x = {}
    for c in range(CHUNKS):
        rows = pl.ds(CHUNK * c, CHUNK)
        for k in ORDER8:
            copy = send(
                part.at[lax.rem(t + k, NT), rows], xbuf.at[k - 1, rows], xs.at[k - 1, c], xr.at[k - 1, c], t_peer(k)
            )
            sent.append(copy)
            got_x[k, c] = copy
    got_y = {}
    for c in range(CHUNKS):
        rows = pl.ds(CHUNK * c, CHUNK)
        total = part[t, rows]
        for k in reversed(ORDER8):
            got_x[k, c].wait_recv()
            total = total + xbuf[k - 1, rows]
        ybuf[y, rows] = total
        for k in ORDER8:
            copy = send(ybuf.at[y, rows], ybuf.at[y, rows], ys.at[k - 1, c], yr.at[k - 1, c], y_peer(k))
            sent.append(copy)
            got_y[k, c] = copy
    got_p = []
    for c in range(CHUNKS):
        rows = pl.ds(CHUNK * c, CHUNK)
        for k in reversed(ORDER8):
            got_y[k, c].wait_recv()
        total = ybuf[0, rows]
        for i in range(1, NY):
            total = total + ybuf[i, rows]
        pfull[t, rows] = total
        for k in ORDER8:
            copy = send(pfull.at[t, rows], pfull.at[t, rows], ps.at[k - 1, c], pr.at[k - 1, c], t_peer(k))
            sent.append(copy)
            got_p.append(copy)
    for copy in got_p:
        copy.wait_recv()

    left = jnp.concatenate([pfull[i] for i in range(NT)], axis=0)
    p_out[...] = left
    left_t = left.T

    blocks = jnp.dot(left_t, left, precision=HIGHEST, preferred_element_type=F32)
    lane8 = lax.broadcasted_iota(jnp.int32, (8, 128), 1)
    tile = jnp.zeros((8, 128), F32)
    for q in range(RANK // 8):
        rows8 = None
        for j in range(GROUPS):
            band = blocks[RANK * j + 8 * q : RANK * j + 8 * q + 8, :]
            band = jnp.where(lax.div(lane8, RANK) == j, band, 0.0)
            rows8 = band if rows8 is None else rows8 + band
        rows8 = rows8 + pltpu.roll(rows8, 64, 1)
        rows8 = rows8 + pltpu.roll(rows8, 32, 1)
        tile = jnp.where(lax.div(lane8, RANK) == q, rows8, tile)
    gbuf[z] = tile
    got_g = []
    for k in ORDER12:
        copy = send(gbuf.at[z], gbuf.at[z], gs.at[k - 1], gr.at[k - 1], z_peer(k))
        sent.append(copy)
        got_g.append(copy)

    bands = []
    for j in range(GROUPS):
        bands.append(left_t[RANK * j : RANK * (j + 1), : GROUP_ROWS if j < GROUPS - 1 else HALF])
    lt = jnp.concatenate(bands, axis=1)
    lhs = jnp.concatenate(split3(lt * (1.0 / NY)), axis=0)
    right = jnp.dot(lhs, gv[...], preferred_element_type=F32) + jnp.dot(
        lhs, ev[...], preferred_element_type=F32
    )
    right = right[:RANK] + (right[RANK : 2 * RANK] + right[2 * RANK :])
    for i in range(NY):
        q, h = i // 2, i % 2
        rpart[i] = right[8 * q : 8 * q + 8, RCOLS * h : RCOLS * (h + 1)]
    got_r = {}
    for k in ORDER8:
        copy = send(rpart.at[lax.rem(y + k, NY)], rsbuf.at[k - 1], rs.at[k - 1], rr.at[k - 1], y_peer(k))
        sent.append(copy)
        got_r[k] = copy
    total = rpart[y]
    for k in reversed(ORDER8):
        got_r[k].wait_recv()
        total = total + rsbuf[k - 1]
    zbuf[z] = total
    got_z = []
    for k in ORDER12:
        copy = send(zbuf.at[z], zbuf.at[z], zs.at[k - 1], zr.at[k - 1], z_peer(k))
        sent.append(copy)
        got_z.append(copy)

    for copy in got_g:
        copy.wait_recv()
    tile = gbuf[0]
    for i in range(1, NZ):
        tile = tile + gbuf[i]
    rows = [tile] + [pltpu.roll(tile, 128 - 32 * q, 1) for q in range(1, RANK // 8)]
    l_out[...] = inverse_lower(jnp.concatenate(rows, axis=0))

    for copy in got_z:
        copy.wait_recv()
    total = zbuf[0]
    for i in range(1, NZ):
        total = total + zbuf[i]
    rfull[y] = total
    got_f = []
    for k in ORDER8:
        copy = send(rfull.at[y], rfull.at[y], fs.at[k - 1], fr.at[k - 1], y_peer(k))
        sent.append(copy)
        got_f.append(copy)
    for copy in got_f:
        copy.wait_recv()
    for i in range(NY):
        q, h = i // 2, i % 2
        rt_out[8 * q : 8 * q + 8, RCOLS * h : RCOLS * (h + 1)] = rfull[i]
    for copy in sent:
        copy.wait_send()


def update_kernel(g_hbm, e_hbm, p_ref, rt_ref, l_ref, err_hbm, nb_ref, gv, ev, ov, load_sem, out_sem):
    blocks = ROWS // HALF
    loads = []
    for b in range(blocks):
        rows = pl.ds(HALF * b, HALF)
        pair = [
            pltpu.make_async_copy(g_hbm.at[rows], gv.at[rows], load_sem.at[0, b]),
            pltpu.make_async_copy(e_hbm.at[rows], ev.at[rows], load_sem.at[1, b]),
        ]
        for copy in pair:
            copy.start()
        loads.append(pair)
    inv = l_ref[...]
    basis_t = jnp.dot(inv[:, :RANK], rt_ref[...], precision=HIGHEST, preferred_element_type=F32)
    nb_ref[...] = basis_t
    lane = lax.broadcasted_iota(jnp.int32, (RANK, 128), 1)
    diag = jnp.concatenate(
        [jnp.where(lax.div(lane, RANK) == j, inv, 0.0) for j in range(GROUPS)], axis=0
    )
    left_basis = lax.dot_general(
        p_ref[...], diag, (((1,), (1,)), ((), ())), precision=HIGHEST, preferred_element_type=F32
    )
    b_hi, b_lo = split2(left_basis)
    lhs = jnp.concatenate([b_hi, b_lo], axis=1)
    n_hi, n_lo = split2(basis_t)
    stores = []
    for b in range(blocks):
        j, h = b // 2, b % 2
        hi = row_bands(n_hi, j)
        rebuilt = jnp.dot(
            lhs[HALF * h : HALF * (h + 1)], jnp.concatenate([hi, hi], axis=0), preferred_element_type=F32
        ) + jnp.dot(b_hi[HALF * h : HALF * (h + 1)], row_bands(n_lo, j), preferred_element_type=F32)
        for copy in loads[b]:
            copy.wait()
        sl = slice(HALF * b, HALF * (b + 1))
        merged = gv[sl, :].astype(F32) + ev[sl, :].astype(F32)
        ov[sl, :] = (merged - rebuilt).astype(BF16)
        rows = pl.ds(HALF * b, HALF)
        copy = pltpu.make_async_copy(ov.at[rows], err_hbm.at[rows], out_sem.at[b])
        copy.start()
        stores.append(copy)
    for copy in stores:
        copy.wait()


def on_device(gradients, error_buffer, warm_basis):
    g, e = gradients[0], error_buffer[0]
    vmem = pl.BlockSpec(memory_space=pltpu.VMEM)
    anyspace = pl.BlockSpec(memory_space=pl.ANY)
    dma = pltpu.SemaphoreType.DMA
    left, right_t, inv = pl.pallas_call(
        comm_kernel,
        name="factors",
        out_shape=(
            jax.ShapeDtypeStruct((GROUP_ROWS, 128), F32),
            jax.ShapeDtypeStruct((RANK, COLS), F32),
            jax.ShapeDtypeStruct((RANK, 128), F32),
        ),
        in_specs=[anyspace, anyspace, vmem],
        out_specs=(vmem, vmem, vmem),
        scratch_shapes=[
            pltpu.VMEM((ROWS, COLS), BF16),
            pltpu.VMEM((ROWS, COLS), BF16),
            pltpu.VMEM((NT, PIECE, 128), F32),
            pltpu.VMEM((NT - 1, PIECE, 128), F32),
            pltpu.VMEM((NY, PIECE, 128), F32),
            pltpu.VMEM((NT, PIECE, 128), F32),
            pltpu.VMEM((NY, 8, RCOLS), F32),
            pltpu.VMEM((NY - 1, 8, RCOLS), F32),
            pltpu.VMEM((NZ, 8, RCOLS), F32),
            pltpu.VMEM((NZ, 8, 128), F32),
            pltpu.VMEM((NY, 8, RCOLS), F32),
            dma((2, GROUPS)),
            dma((NT - 1, CHUNKS)), dma((NT - 1, CHUNKS)),
            dma((NY - 1, CHUNKS)), dma((NY - 1, CHUNKS)),
            dma((NT - 1, CHUNKS)), dma((NT - 1, CHUNKS)),
            dma((NZ - 1,)), dma((NZ - 1,)),
            dma((NY - 1,)), dma((NY - 1,)),
            dma((NZ - 1,)), dma((NZ - 1,)),
            dma((NY - 1,)), dma((NY - 1,)),
        ],
        compiler_params=pltpu.CompilerParams(collective_id=0, has_side_effects=True),
    )(g, e, warm_basis.T)
    new_errors, basis_t = pl.pallas_call(
        update_kernel,
        name="update",
        out_shape=(
            jax.ShapeDtypeStruct((ROWS, COLS), BF16),
            jax.ShapeDtypeStruct((RANK, COLS), F32),
        ),
        in_specs=[anyspace, anyspace, vmem, vmem, vmem],
        out_specs=(anyspace, vmem),
        scratch_shapes=[
            pltpu.VMEM((ROWS, COLS), BF16),
            pltpu.VMEM((ROWS, COLS), BF16),
            pltpu.VMEM((ROWS, COLS), BF16),
            dma((2, ROWS // HALF)),
            dma((ROWS // HALF,)),
        ],
    )(g, e, left, right_t, inv)
    return new_errors[None], basis_t.T


def solution(mesh):
    placed = (P("dp", None, "tensor"), P("dp", None, "tensor"), P("tensor", None))
    return jax.shard_map(
        on_device,
        mesh=mesh,
        in_specs=placed,
        out_specs=(P("dp", None, "tensor"), P("tensor", None)),
        check_vma=False,
    )
```

time: 752 us -> 59.9 us (0.08)
  waiting for transfers between devices: 699 us -> 0 us
  Pallas kernels: 0 us -> 58.4 us
  matrix products: 19.8 us -> 0 us
  between operations: 14.1 us -> 0.64 us
  other arithmetic: 7.53 us -> 0 us
    psum x2 -> x0, waiting for transfers between devices: 699 us -> none  [the longest x1 487 us: on_device(): left_factor = lax.psum(padded, ('dp', 'tensor')) / REPLICAS]
    pallas_call x0 -> x2, Pallas kernels: none -> 58.4 us  [the longest x1 52.6 us: on_device(): pl.pallas_call(comm_kernel, name='factors', out_shape=(jax.ShapeDtypeStru...]
    dot_general x4 -> x0, matrix products: 16.1 us -> none  [the longest x1 4.9 us: on_device(): lax.dot_general(basis_own, new_basis, (((1,), (1,)), ((), ())), precision...]
  transfers between devices with their start and end apart: 2 -> 0, of which waited for: 2 -> 0; matrix products, arithmetic and copies ran while one was open for 0% -> 0% of each run, Pallas kernels for 0% -> 0%
where the time goes in v1:
time: 59.9 us; the launch traced here: 59 us
  Pallas kernels  58.4 us (97%)
  between operations  0.64 us (1%)
    pallas_call x1, Pallas kernels, on_device(): pl.pallas_call(comm_kernel, name='factors', out_shape=(jax.ShapeDtypeStru...  52.6 us
    pallas_call x1, Pallas kernels, on_device(): pl.pallas_call(update_kernel, name='update', out_shape=(jax.ShapeDtypeStr...  5.73 us

profile of v1, /device:TPU:1, one launch (start us, length us, event | category | flops | bytes accessed | tf_op | source)
XLA Modules:
  0.0 59.0 jit_solution(9155095479593617592)
XLA Ops:
  0.6 52.6 %factors.1 = (f32[384,128]{1,0:T(8,128)}, f32[32,512]{1,0:T(8,128)}, f32[32,128]{1,0:T(8,128)}) custom-call(bf16[1344,512]{1,0:T(8,128)(2,1)} %bitcast.5, bf16[1344,512]{1,0:T(8,128)(2,1)} %bitcast.7, f32[32,512]{1,0:T(8,128)} %bitcast.9), custom_call_target="tpu_custom_call" | custom-call | tf_op jit(solution)/shard_map/factors/pallas_call | solution.py:302
  53.3 5.7 %update.1 = (bf16[1344,512]{1,0:T(8,128)(2,1)}, f32[32,512]{1,0:T(8,128)}) custom-call(bf16[1344,512]{1,0:T(8,128)(2,1)} %bitcast.6, bf16[1344,512]{1,0:T(8,128)(2,1)} %bitcast.8, f32[384,128]{1,0:T(8,128)} %get-tuple-element.7.p_ref, f32[32,512]{1,0:T(8,128)} %get-tuple-element.8.rt_ref, f32[32,128]{1,0:T(8,128)} %get-tuple-element.9.l_ref), custom_call_target="tpu_custom_call" | custom-call | tf_op jit(solution)/shard_map/update/pallas_call | solution.py:335

commit v2 on v1

v2 whole, which is shorter than its diff:
```python
import jax
import jax.numpy as jnp
from jax import lax
from jax.experimental import pallas as pl
from jax.experimental.pallas import tpu as pltpu
from jax.sharding import PartitionSpec as P

MESH = pl.DeviceIdType.MESH
HIGHEST = lax.Precision.HIGHEST
F32 = jnp.float32
BF16 = jnp.bfloat16

NY = 8
NZ = 12
NT = 8
ROWS = 1344
COLS = 512
RANK = 32
GROUPS = 4
GROUP_ROWS = 384
HALF = 192
PIECE = GROUP_ROWS // NT
CHUNKS = 3
CHUNK = PIECE // CHUNKS
RCHUNKS = 2

ORDER8 = (4, 3, 5, 2, 6, 1, 7)
ORDER12 = (6, 5, 7, 4, 8, 3, 9, 2, 10, 1, 11)


def split2(x):
    hi = x.astype(BF16)
    return hi, (x - hi.astype(F32)).astype(BF16)


def split3(x):
    hi = x.astype(BF16)
    rest = x - hi.astype(F32)
    mid = rest.astype(BF16)
    return hi, mid, (rest - mid.astype(F32)).astype(BF16)


def row_bands(x, group):
    n = x.shape[1]
    parts = []
    if group:
        parts.append(jnp.zeros((RANK * group, n), x.dtype))
    parts.append(x)
    if group < GROUPS - 1:
        parts.append(jnp.zeros((RANK * (GROUPS - 1 - group), n), x.dtype))
    return jnp.concatenate(parts, axis=0)


def inverse_lower(gram):
    lane = lax.broadcasted_iota(jnp.int32, (RANK, 128), 1)
    row = lax.broadcasted_iota(jnp.int32, (RANK, 128), 0)
    a = jnp.where(lane < RANK, gram, jnp.where(lane == row + RANK, 1.0, 0.0))
    for k in range(RANK - 1):
        pivot = a[k : k + 1, :]
        factor = a[:, k : k + 1] * (1.0 / pivot[:, k : k + 1])
        factor = jnp.where(row[:, :1] > k, factor, 0.0)
        a = a - factor * pivot
    diagonal = jnp.sum(jnp.where(lane == row, a, 0.0), axis=1, keepdims=True)
    inv = a * lax.rsqrt(diagonal)
    inv = jnp.where((lane >= RANK) & (lane < 2 * RANK), inv, 0.0)
    inv = inv + pltpu.roll(inv, 2 * RANK, 1)
    return inv + pltpu.roll(inv, RANK, 1)


def factors_kernel(
    g_hbm, e_hbm, wt_hbm, gv, ev, lhs_ref, nb_ref,
    wt, part, xbuf, ybuf, pfull, rpart, rsbuf, zbuf, gbuf, rfull,
    load_sem, send_sem, xr, yr, pr, gr, rr, zr, fr,
):
    dp = lax.axis_index("dp")
    t = lax.axis_index("tensor")
    y = lax.div(dp, NZ)
    z = lax.rem(dp, NZ)

    def t_peer(k):
        return {"dp": dp, "tensor": lax.rem(t + k, NT)}

    def y_peer(k):
        return {"dp": lax.rem(y + k, NY) * NZ + z, "tensor": t}

    def z_peer(k):
        return {"dp": y * NZ + lax.rem(z + k, NZ), "tensor": t}

    def send(src, dst, ssem, rsem, peer):
        copy = pltpu.make_async_remote_copy(
            src_ref=src, dst_ref=dst, send_sem=ssem, recv_sem=rsem, device_id=peer, device_id_type=MESH
        )
        copy.start()

    def arrived(ref, sem):
        pltpu.make_async_remote_copy(
            src_ref=ref, dst_ref=ref, send_sem=send_sem.at[0], recv_sem=sem, device_id=t_peer(1), device_id_type=MESH
        ).wait_recv()

    def left_here(ref, sem):
        pltpu.make_async_remote_copy(
            src_ref=ref, dst_ref=ref, send_sem=sem, recv_sem=xr.at[0], device_id=t_peer(1), device_id_type=MESH
        ).wait_send()

    barrier = pltpu.get_barrier_semaphore()
    for k in ORDER8:
        pl.semaphore_signal(barrier, inc=1, device_id=y_peer(k), device_id_type=MESH)
    wt_load = pltpu.make_async_copy(wt_hbm, wt, load_sem.at[2 * GROUPS])
    wt_load.start()
    loads = []
    for j in range(GROUPS):
        rows = pl.ds(GROUP_ROWS * j, GROUP_ROWS if j < GROUPS - 1 else HALF)
        pair = [
            pltpu.make_async_copy(g_hbm.at[rows], gv.at[rows], load_sem.at[2 * j]),
            pltpu.make_async_copy(e_hbm.at[rows], ev.at[rows], load_sem.at[2 * j + 1]),
        ]
        for copy in pair:
            copy.start()
        loads.append(pair)
    for k in ORDER12:
        pl.semaphore_signal(barrier, inc=1, device_id=z_peer(k), device_id_type=MESH)
    for k in ORDER8:
        pl.semaphore_signal(barrier, inc=1, device_id=t_peer(k), device_id_type=MESH)

    wt_load.wait()
    w_hi, w_lo = split2(wt[...] * (1.0 / NY))
    acc = [None, None]
    nt_dims = (((1,), (1,)), ((), ()))
    for j in range(GROUPS):
        weights = jnp.concatenate([row_bands(w_hi, j), row_bands(w_lo, j)], axis=0)
        for copy in loads[j]:
            copy.wait()
        for h in range(2 if j < GROUPS - 1 else 1):
            start = GROUP_ROWS * j + HALF * h
            for ref in (gv, ev):
                term = lax.dot_general(
                    ref[start : start + HALF, :], weights, nt_dims, preferred_element_type=F32
                )
                acc[h] = term if acc[h] is None else acc[h] + term
    for h in range(2):
        packed = acc[h][:, :128] + acc[h][:, 128:]
        for i in range(NT // 2):
            part[h * (NT // 2) + i] = packed[PIECE * i : PIECE * (i + 1)]

    pl.semaphore_wait(barrier, NZ + NY + NT - 3)

    for c in range(CHUNKS):
        rows = pl.ds(CHUNK * c, CHUNK)
        for k in ORDER8:
            send(part.at[lax.rem(t + k, NT), rows], xbuf.at[k - 1, rows], send_sem.at[0], xr.at[c], t_peer(k))
    for c in range(CHUNKS):
        rows = pl.ds(CHUNK * c, CHUNK)
        arrived(xbuf.at[:, rows], xr.at[c])
        total = part[t, rows]
        for i in range(NT - 1):
            total = total + xbuf[i, rows]
        ybuf[y, rows] = total
        for k in ORDER8:
            send(ybuf.at[y, rows], ybuf.at[y, rows], send_sem.at[1], yr.at[c], y_peer(k))
    for c in range(CHUNKS):
        rows = pl.ds(CHUNK * c, CHUNK)
        arrived(ybuf.at[pl.ds(0, NY - 1), rows], yr.at[c])
        total = ybuf[0, rows]
        for i in range(1, NY):
            total = total + ybuf[i, rows]
        pfull[t, rows] = total
        for k in ORDER8:
            send(pfull.at[t, rows], pfull.at[t, rows], send_sem.at[2], pr, t_peer(k))
    arrived(pfull.at[pl.ds(0, NT - 1)], pr)

    left = jnp.concatenate([pfull[i] for i in range(NT)], axis=0)
    left_t = left.T

    bands = []
    for j in range(GROUPS):
        bands.append(left_t[RANK * j : RANK * (j + 1), : GROUP_ROWS if j < GROUPS - 1 else HALF])
    lt = jnp.concatenate(bands, axis=1)
    lhs = jnp.concatenate(split3(lt * (1.0 / NY)), axis=0)
    right = jnp.dot(lhs, gv[...], preferred_element_type=F32) + jnp.dot(
        lhs, ev[...], preferred_element_type=F32
    )
    right = right[:RANK] + (right[RANK : 2 * RANK] + right[2 * RANK :])
    for c in range(RCHUNKS):
        for i in range(NY):
            q, h = i // 2, 2 * (i % 2) + c
            rpart[c, i] = right[8 * q : 8 * q + 8, 128 * h : 128 * (h + 1)]
    for c in range(RCHUNKS):
        for k in ORDER8:
            send(rpart.at[c, lax.rem(y + k, NY)], rsbuf.at[c, k - 1], send_sem.at[3], rr.at[c], y_peer(k))

    blocks = jnp.dot(left_t, left, precision=HIGHEST, preferred_element_type=F32)
    lane8 = lax.broadcasted_iota(jnp.int32, (8, 128), 1)
    tile = jnp.zeros((8, 128), F32)
    for q in range(RANK // 8):
        rows8 = None
        for j in range(GROUPS):
            band = blocks[RANK * j + 8 * q : RANK * j + 8 * q + 8, :]
            band = jnp.where(lax.div(lane8, RANK) == j, band, 0.0)
            rows8 = band if rows8 is None else rows8 + band
        rows8 = rows8 + pltpu.roll(rows8, 64, 1)
        rows8 = rows8 + pltpu.roll(rows8, 32, 1)
        tile = jnp.where(lax.div(lane8, RANK) == q, rows8, tile)
    gbuf[z] = tile
    for k in ORDER12:
        send(gbuf.at[z], gbuf.at[z], send_sem.at[4], gr, z_peer(k))

    for c in range(RCHUNKS):
        arrived(rsbuf.at[c], rr.at[c])
        total = rpart[c, y]
        for i in range(NY - 1):
            total = total + rsbuf[c, i]
        zbuf[c, z] = total
        for k in ORDER12:
            send(zbuf.at[c, z], zbuf.at[c, z], send_sem.at[5], zr.at[c], z_peer(k))

    arrived(gbuf.at[pl.ds(0, NZ - 1)], gr)
    tile = gbuf[0]
    for i in range(1, NZ):
        tile = tile + gbuf[i]
    rows = [tile] + [pltpu.roll(tile, 128 - 32 * q, 1) for q in range(1, RANK // 8)]
    inv = inverse_lower(jnp.concatenate(rows, axis=0))

    for c in range(RCHUNKS):
        arrived(zbuf.at[c, pl.ds(0, NZ - 1)], zr.at[c])
        total = zbuf[c, 0]
        for i in range(1, NZ):
            total = total + zbuf[c, i]
        rfull[c, y] = total
        for k in ORDER8:
            send(rfull.at[c, y], rfull.at[c, y], send_sem.at[6], fr, y_peer(k))

    lane = lax.broadcasted_iota(jnp.int32, (RANK, 128), 1)
    diag = jnp.concatenate(
        [jnp.where(lax.div(lane, RANK) == j, inv, 0.0) for j in range(GROUPS)], axis=0
    )
    left_basis = lax.dot_general(left, diag, nt_dims, precision=HIGHEST, preferred_element_type=F32)
    b_hi = left_basis.astype(BF16).astype(F32)
    b_lo = left_basis - b_hi
    wide = lax.broadcasted_iota(jnp.int32, (GROUP_ROWS, 128), 1)
    for j in range(GROUPS):
        n = GROUP_ROWS if j < GROUPS - 1 else HALF
        first = pltpu.roll(b_hi[:n], (128 - RANK * j) % 128, 1) if j else b_hi[:n]
        second = pltpu.roll(b_lo[:n], (128 + RANK - RANK * j) % 128, 1) if j != 1 else b_lo[:n]
        third = pltpu.roll(b_hi[:n], (128 + 2 * RANK - RANK * j) % 128, 1) if j != 2 else b_hi[:n]
        mixed = jnp.where(wide[:n] < RANK, first, jnp.where(wide[:n] < 2 * RANK, second, third))
        mixed = jnp.where(wide[:n] < 3 * RANK, mixed, 0.0)
        lhs_ref[GROUP_ROWS * j : GROUP_ROWS * j + n] = mixed.astype(BF16)
    i_hi, i_mid, i_lo = split3(inv[:, :RANK])
    inv_lhs = jnp.concatenate([i_hi, i_hi, i_mid, i_hi, i_mid, i_lo], axis=1)

    arrived(rfull.at[:, pl.ds(0, NY - 1)], fr)

    rt = jnp.concatenate(
        [jnp.concatenate([rfull[h % 2, 2 * q + h // 2] for h in range(4)], axis=1) for q in range(RANK // 8)],
        axis=0,
    )
    r_hi, r_mid, r_lo = split3(rt)
    basis_t = jnp.dot(
        inv_lhs, jnp.concatenate([r_hi, r_mid, r_hi, r_lo, r_mid, r_hi], axis=0), preferred_element_type=F32
    )
    nb_ref[...] = basis_t
    left_here(xbuf, send_sem.at[0])
    left_here(xbuf, send_sem.at[1])
    left_here(xbuf, send_sem.at[2])
    left_here(rsbuf, send_sem.at[3])
    left_here(gbuf.at[pl.ds(0, NZ - 1)], send_sem.at[4])
    left_here(zbuf.at[:, pl.ds(0, NZ - 1)], send_sem.at[5])
    left_here(rsbuf, send_sem.at[6])


def update_kernel(gv, ev, lhs_ref, basis_ref, err_hbm, nb_hbm, out, sem):
    blocks = ROWS // HALF
    stores = [pltpu.make_async_copy(basis_ref, nb_hbm, sem.at[blocks])]
    stores[0].start()
    n_hi, n_lo = split2(basis_ref[...])
    rhs = jnp.concatenate([n_hi, n_hi, n_lo, jnp.zeros_like(n_lo)], axis=0)
    for b in range(blocks):
        sl = slice(HALF * b, HALF * (b + 1))
        rebuilt = jnp.dot(lhs_ref[sl, :], rhs, preferred_element_type=F32)
        merged = gv[sl, :].astype(F32) + ev[sl, :].astype(F32)
        out[sl, :] = (merged - rebuilt).astype(BF16)
        rows = pl.ds(HALF * b, HALF)
        copy = pltpu.make_async_copy(out.at[rows], err_hbm.at[rows], sem.at[b])
        copy.start()
        stores.append(copy)
    for copy in stores:
        copy.wait()


def on_device(gradients, error_buffer, warm_basis):
    vmem = pl.BlockSpec(memory_space=pltpu.VMEM)
    anyspace = pl.BlockSpec(memory_space=pl.ANY)
    dma = pltpu.SemaphoreType.DMA
    wide = (ROWS, COLS)
    kept = pl.pallas_call(
        factors_kernel,
        name="factors",
        out_shape=(
            pltpu.VMEM(wide, BF16),
            pltpu.VMEM(wide, BF16),
            pltpu.VMEM((ROWS, 128), BF16),
            pltpu.VMEM((RANK, COLS), F32),
        ),
        in_specs=[anyspace, anyspace, anyspace],
        out_specs=(vmem, vmem, vmem, vmem),
        scratch_shapes=[
            pltpu.VMEM((RANK, COLS), F32),
            pltpu.VMEM((NT, PIECE, 128), F32),
            pltpu.VMEM((NT - 1, PIECE, 128), F32),
            pltpu.VMEM((NY, PIECE, 128), F32),
            pltpu.VMEM((NT, PIECE, 128), F32),
            pltpu.VMEM((RCHUNKS, NY, 8, 128), F32),
            pltpu.VMEM((RCHUNKS, NY - 1, 8, 128), F32),
            pltpu.VMEM((RCHUNKS, NZ, 8, 128), F32),
            pltpu.VMEM((NZ, 8, 128), F32),
            pltpu.VMEM((RCHUNKS, NY, 8, 128), F32),
            dma((2 * GROUPS + 1,)),
            dma((7,)),
            dma((CHUNKS,)), dma((CHUNKS,)), dma,
            dma, dma((RCHUNKS,)), dma((RCHUNKS,)), dma,
        ],
        compiler_params=pltpu.CompilerParams(
            collective_id=0, has_side_effects=True, vmem_limit_bytes=24 * 1024 * 1024
        ),
    )(*(pltpu.with_memory_space_constraint(x, pltpu.HBM) for x in (gradients[0], error_buffer[0], warm_basis.T)))
    new_errors, basis_t = pl.pallas_call(
        update_kernel,
        name="update",
        out_shape=(jax.ShapeDtypeStruct(wide, BF16), jax.ShapeDtypeStruct((RANK, COLS), F32)),
        in_specs=[vmem, vmem, vmem, vmem],
        out_specs=(anyspace, anyspace),
        scratch_shapes=[pltpu.VMEM(wide, BF16), dma((ROWS // HALF + 1,))],
        compiler_params=pltpu.CompilerParams(vmem_limit_bytes=24 * 1024 * 1024),
    )(*(pltpu.with_memory_space_constraint(x, pltpu.VMEM) for x in kept))
    return new_errors[None], basis_t.T


def solution(mesh):
    placed = (P("dp", None, "tensor"), P("dp", None, "tensor"), P("tensor", None))
    return jax.shard_map(
        on_device,
        mesh=mesh,
        in_specs=placed,
        out_specs=(P("dp", None, "tensor"), P("tensor", None)),
        check_vma=False,
    )
```

time: 59.9 us -> 53 us (0.88)
  Pallas kernels: 58.4 us -> 51.8 us
    pallas_call x1, Pallas kernels: 5.73 us -> 1.33 us  [on_device(): pl.pallas_call(update_kernel, name='update', out_shape=(jax.ShapeDtypeStr...]
    pallas_call x1, Pallas kernels: 52.6 us -> 50.5 us  [on_device(): pl.pallas_call(factors_kernel, name='factors', out_shape=(pltpu.VMEM(wide...]
where the time goes in v2:
time: 53 us; the launch traced here: 52.5 us
  Pallas kernels  51.8 us (98%)
  between operations  0.64 us (1%)
    pallas_call x1, Pallas kernels, on_device(): pl.pallas_call(factors_kernel, name='factors', out_shape=(pltpu.VMEM(wide...  50.5 us
    pallas_call x1, Pallas kernels, on_device(): pl.pallas_call(update_kernel, name='update', out_shape=(jax.ShapeDtypeStr...  1.33 us

profile of v2, /device:TPU:1, one launch (start us, length us, event | category | flops | bytes accessed | tf_op | source)
XLA Modules:
  0.0 52.5 jit_solution(9333349983765753294)
XLA Ops:
  0.6 50.5 %factors.1 = (bf16[1344,512]{1,0:T(8,128)(2,1)S(1)}, bf16[1344,512]{1,0:T(8,128)(2,1)S(1)}, bf16[1344,128]{1,0:T(8,128)(2,1)S(1)}, f32[32,512]{1,0:T(8,128)S(1)}) custom-call(bf16[1344,512]{1,0:T(8,128)(2,1)} %bitcast.5, bf16[1344,512]{1,0:T(8,128)(2,1)} %bitcast.6, f32[32,512]{1,0:T(8,128)} %bitcast.7), custom_call_target="tpu_custom_call" | custom-call | tf_op jit(solution)/shard_map/factors/pallas_call | solution.py:295
  51.1 1.3 %update.1 = (bf16[1344,512]{1,0:T(8,128)(2,1)}, f32[32,512]{1,0:T(8,128)}) custom-call(bf16[1344,512]{1,0:T(8,128)(2,1)S(1)} %get-tuple-element.8.gv, bf16[1344,512]{1,0:T(8,128)(2,1)S(1)} %get-tuple-element.9.ev, bf16[1344,128]{1,0:T(8,128)(2,1)S(1)} %get-tuple-element.10.lhs_ref, f32[32,512]{1,0:T(8,128)S(1)} %get-tuple-element.11.basis_ref), custom_call_target="tpu_custom_call" | custom-call | tf_op jit(solution)/shard_map/update/pallas_call | solution.py:326

commit v3 on v2

v3 whole, which is shorter than its diff:
```python
import functools

import jax
import jax.numpy as jnp
from jax import lax
from jax.experimental import pallas as pl
from jax.experimental.pallas import tpu as pltpu
from jax.sharding import PartitionSpec as P

MESH = pl.DeviceIdType.MESH
HIGHEST = lax.Precision.HIGHEST
F32 = jnp.float32
BF16 = jnp.bfloat16

NY = 8
NZ = 12
NX = 4
ROWS = 1344
COLS = 512
RANK = 32
GROUPS = 4
GROUP_ROWS = 384
HALF = 192
CHUNKS = 3
PIECE = 128 // NX
RCHUNKS = 2

ORDER4 = (2, 1, 3)
ORDER8 = (4, 3, 5, 2, 6, 1, 7)
ORDER12 = (1, 11, 2, 10, 3, 9, 4, 8, 5, 7, 6)


def chunk_rows(c):
    rows = []
    for j in range(GROUPS):
        length = min(128, (GROUP_ROWS if j < GROUPS - 1 else HALF) - 128 * c)
        if length > 0:
            rows.append((j, GROUP_ROWS * j + 128 * c, length))
    return rows


def split2(x):
    hi = x.astype(BF16)
    return hi, (x - hi.astype(F32)).astype(BF16)


def split3(x):
    hi = x.astype(BF16)
    rest = x - hi.astype(F32)
    mid = rest.astype(BF16)
    return hi, mid, (rest - mid.astype(F32)).astype(BF16)


def row_bands(x, group):
    n = x.shape[1]
    parts = []
    if group:
        parts.append(jnp.zeros((RANK * group, n), x.dtype))
    parts.append(x)
    if group < GROUPS - 1:
        parts.append(jnp.zeros((RANK * (GROUPS - 1 - group), n), x.dtype))
    return jnp.concatenate(parts, axis=0)


def inverse_lower(gram):
    lane = lax.broadcasted_iota(jnp.int32, (RANK, 128), 1)
    row = lax.broadcasted_iota(jnp.int32, (RANK, 128), 0)
    a = jnp.where(lane < RANK, gram, jnp.where(lane == row + RANK, 1.0, 0.0))
    for k in range(RANK - 1):
        pivot = a[k : k + 1, :]
        factor = a[:, k : k + 1] * (1.0 / pivot[:, k : k + 1])
        factor = jnp.where(row[:, :1] > k, factor, 0.0)
        a = a - factor * pivot
    diagonal = jnp.sum(jnp.where(lane == row, a, 0.0), axis=1, keepdims=True)
    inv = a * lax.rsqrt(diagonal)
    inv = jnp.where((lane >= RANK) & (lane < 2 * RANK), inv, 0.0)
    inv = inv + pltpu.roll(inv, 2 * RANK, 1)
    return inv + pltpu.roll(inv, RANK, 1)


def factors_kernel(
    g_hbm, e_hbm, wt_hbm, gv, ev, lhs_ref, nb_ref,
    wt, part, xbuf, ybuf, pfull, rpart, rbuf0, rbuf1, zbuf, zsum, gbuf, gsum, rfull,
    load_sem, send_sem, xr, yr, pr, gr, gm, rr0, rr1, zr, fr, reach,
):
    dp = lax.axis_index("dp")
    t = lax.axis_index("tensor")
    y = lax.div(dp, NZ)
    z = lax.rem(dp, NZ)
    x = lax.div(t, 2)
    core = lax.rem(t, 2)

    def x_peer(k, c):
        return {"dp": dp, "tensor": lax.rem(x + k, NX) * 2 + c}

    def y_peer(k, c):
        return {"dp": lax.rem(y + k, NY) * NZ + z, "tensor": x * 2 + c}

    def z_peer(k):
        return {"dp": y * NZ + lax.rem(z + k, NZ), "tensor": t}

    def send(src, dst, ssem, rsem, peer):
        pltpu.make_async_remote_copy(
            src_ref=src, dst_ref=dst, send_sem=ssem, recv_sem=rsem, device_id=peer, device_id_type=MESH
        ).start()

    def arrived(ref, sem):
        pltpu.make_async_remote_copy(
            src_ref=ref, dst_ref=ref, send_sem=send_sem.at[0], recv_sem=sem, device_id=x_peer(1, core), device_id_type=MESH
        ).wait_recv()

    def left_here(ref, sem):
        pltpu.make_async_remote_copy(
            src_ref=ref, dst_ref=ref, send_sem=sem, recv_sem=xr.at[0], device_id=x_peer(1, core), device_id_type=MESH
        ).wait_send()

    def signal(sem, peer):
        pl.semaphore_signal(sem, inc=1, device_id=peer, device_id_type=MESH)

    on_core0 = functools.partial(pl.when, core == 0)
    on_core1 = functools.partial(pl.when, core == 1)

    wt_load = pltpu.make_async_copy(wt_hbm, wt, load_sem.at[2 * GROUPS])
    wt_load.start()
    loads = []
    for j in range(GROUPS):
        rows = pl.ds(GROUP_ROWS * j, GROUP_ROWS if j < GROUPS - 1 else HALF)
        loads.append(pltpu.make_async_copy(g_hbm.at[rows], gv.at[rows], load_sem.at[2 * j]))
        loads.append(pltpu.make_async_copy(e_hbm.at[rows], ev.at[rows], load_sem.at[2 * j + 1]))
        loads[-2].start()
        loads[-1].start()

    barrier = pltpu.get_barrier_semaphore()

    @on_core1()
    def _():
        for k in ORDER8:
            signal(barrier, y_peer(k, 1))
            signal(barrier, y_peer(k, 0))
        for k in (1, NZ - 1):
            signal(barrier, z_peer(k))
        for k in ORDER4:
            signal(barrier, x_peer(k, 1))
            signal(barrier, x_peer(k, 0))
        signal(barrier, x_peer(0, 0))

    @on_core0()
    def _():
        for k in ORDER8:
            signal(barrier, y_peer(k, 1))
        for k in ORDER4 + (0,):
            signal(barrier, x_peer(k, 1))

    wt_load.wait()
    w_hi, w_lo = split2(wt[...] * (1.0 / NY))
    weights = [jnp.concatenate([row_bands(w_hi, j), row_bands(w_lo, j)], axis=0) for j in range(GROUPS)]
    nt_dims = (((1,), (1,)), ((), ()))
    for c in range(CHUNKS):
        acc = None
        for j, start, length in chunk_rows(c):
            if c == 0:
                loads[2 * j].wait()
                loads[2 * j + 1].wait()
            for ref in (gv, ev):
                term = lax.dot_general(
                    ref[start : start + length, :], weights[j], nt_dims, preferred_element_type=F32
                )
                if acc is None:
                    acc = term
                elif length == 128:
                    acc = acc + term
                else:
                    acc = jnp.concatenate([acc[:length] + term, acc[length:]], axis=0)
        packed = acc[:, :128] + acc[:, 128:]
        for i in range(NX):
            part[c, i] = packed[PIECE * i : PIECE * (i + 1)]
        if c == 0:

            @on_core1()
            def _():
                pl.semaphore_wait(barrier, 2 * (NX - 1) + 1 + 2 * (NY - 1) + 2)
                for k in (1, NZ - 1):
                    signal(reach.at[0], z_peer(k))

            @on_core0()
            def _():
                pl.semaphore_wait(barrier, NX + NY - 1)

        @on_core1()
        def _():
            for k in ORDER4:
                send(part.at[c, lax.rem(x + k, NX)], xbuf.at[c, k - 1], send_sem.at[0], xr.at[c], x_peer(k, 1))

        @on_core0()
        def _():
            for k in ORDER4 + (0,):
                send(part.at[c, lax.rem(x + k, NX)], xbuf.at[c, NX - 1 + k], send_sem.at[0], xr.at[c], x_peer(k, 1))

    @on_core1()
    def _():
        for c in range(CHUNKS):
            arrived(xbuf.at[c], xr.at[c])
            total = part[c, x]
            for i in range(2 * NX - 1):
                total = total + xbuf[c, i]
            ybuf[c, y] = total
            for k in ORDER8:
                send(ybuf.at[c, y], ybuf.at[c, y], send_sem.at[1], yr.at[c], y_peer(k, 1))
        pl.semaphore_wait(reach.at[0], 2)
        for k in (2, NZ - 2):
            signal(reach.at[1], z_peer(k))
        for c in range(CHUNKS):
            if c == 1:
                pl.semaphore_wait(reach.at[1], 2)
                for k in (2, NZ - 2):
                    signal(reach.at[2], z_peer(k))
            arrived(ybuf.at[c, pl.ds(0, NY - 1)], yr.at[c])
            total = ybuf[c, 0]
            for i in range(1, NY):
                total = total + ybuf[c, i]
            pfull[c, x] = total
            for k in ORDER4:
                send(pfull.at[c, x], pfull.at[c, x], send_sem.at[2], pr.at[c], x_peer(k, 0))
                send(pfull.at[c, x], pfull.at[c, x], send_sem.at[2], pr.at[c], x_peer(k, 1))
            send(pfull.at[c, x], pfull.at[c, x], send_sem.at[2], pr.at[c], x_peer(0, 0))

    right = None
    for c in range(CHUNKS):

        @on_core1()
        def _():
            arrived(pfull.at[c, pl.ds(0, NX - 1)], pr.at[c])

        @on_core0()
        def _():
            arrived(pfull.at[c], pr.at[c])

        left_t = jnp.concatenate([pfull[c, i] for i in range(NX)], axis=0).T
        rows = chunk_rows(c)
        lt = jnp.concatenate([left_t[RANK * j : RANK * (j + 1), :length] for j, _, length in rows], axis=1)
        lhs = jnp.concatenate(split3(lt * (1.0 / NY)), axis=0)
        for ref in (gv, ev):
            block = jnp.concatenate([ref[start : start + length, :] for _, start, length in rows], axis=0)
            term = jnp.dot(lhs, block, preferred_element_type=F32)
            right = term if right is None else right + term
    right = right[:RANK] + (right[RANK : 2 * RANK] + right[2 * RANK :])
    for c in range(RCHUNKS):
        for i in range(NY):
            q, h = i // 2, 2 * (i % 2) + c
            rpart[c, i] = right[8 * q : 8 * q + 8, 128 * h : 128 * (h + 1)]
    left = jnp.concatenate([pfull[c, i] for c in range(CHUNKS) for i in range(NX)], axis=0)

    @on_core0()
    def _():
        for c in range(RCHUNKS):
            for k in ORDER8 + (0,):
                send(rpart.at[c, lax.rem(y + k, NY)], rbuf0.at[c, k], send_sem.at[3], rr0.at[c], y_peer(k, 1))
        arrived(gsum, gm)

    @on_core1()
    def _():
        for c in range(RCHUNKS):
            for k in ORDER8:
                send(rpart.at[c, lax.rem(y + k, NY)], rbuf1.at[c, k - 1], send_sem.at[3], rr1.at[c], y_peer(k, 1))

        blocks = jnp.dot(left.T, left, precision=HIGHEST, preferred_element_type=F32)
        lane8 = lax.broadcasted_iota(jnp.int32, (8, 128), 1)
        tile = jnp.zeros((8, 128), F32)
        for q in range(RANK // 8):
            rows8 = None
            for j in range(GROUPS):
                band = blocks[RANK * j + 8 * q : RANK * j + 8 * q + 8, :]
                band = jnp.where(lax.div(lane8, RANK) == j, band, 0.0)
                rows8 = band if rows8 is None else rows8 + band
            rows8 = rows8 + pltpu.roll(rows8, 64, 1)
            rows8 = rows8 + pltpu.roll(rows8, 32, 1)
            tile = jnp.where(lax.div(lane8, RANK) == q, rows8, tile)
        gbuf[z] = tile
        pl.semaphore_wait(reach.at[2], 2)
        for k in ORDER12:
            send(gbuf.at[z], gbuf.at[z], send_sem.at[4], gr, z_peer(k))

        for c in range(RCHUNKS):
            arrived(rbuf1.at[c], rr1.at[c])
            total = rpart[c, y]
            for i in range(NY - 1):
                total = total + rbuf1[c, i]
            zbuf[c, z, 1] = total
            arrived(rbuf0.at[c], rr0.at[c])
            total = rbuf0[c, 0]
            for i in range(1, NY):
                total = total + rbuf0[c, i]
            zbuf[c, z, 0] = total
            for k in ORDER12:
                send(zbuf.at[c, z], zbuf.at[c, z], send_sem.at[5], zr.at[c], z_peer(k))

        arrived(gbuf.at[pl.ds(0, NZ - 1)], gr)
        tile = gbuf[0]
        for i in range(1, NZ):
            tile = tile + gbuf[i]
        gsum[...] = tile
        send(gsum, gsum, send_sem.at[6], gm, x_peer(0, 0))

    tile = gsum[...]
    rows = [tile] + [pltpu.roll(tile, 128 - 32 * q, 1) for q in range(1, RANK // 8)]
    inv = inverse_lower(jnp.concatenate(rows, axis=0))

    @on_core1()
    def _():
        for c in range(RCHUNKS):
            arrived(zbuf.at[c, pl.ds(0, NZ - 1)], zr.at[c])
            total = zbuf[c, 0]
            for i in range(1, NZ):
                total = total + zbuf[c, i]
            zsum[c] = total[0]
            rfull[c, y] = total[1]
            for k in ORDER8:
                send(zsum.at[c], rfull.at[c, y], send_sem.at[7], fr, y_peer(k, 0))
                send(rfull.at[c, y], rfull.at[c, y], send_sem.at[8], fr, y_peer(k, 1))
            send(zsum.at[c], rfull.at[c, y], send_sem.at[7], fr, x_peer(0, 0))

    lane = lax.broadcasted_iota(jnp.int32, (RANK, 128), 1)
    diag = jnp.concatenate(
        [jnp.where(lax.div(lane, RANK) == j, inv, 0.0) for j in range(GROUPS)], axis=0
    )
    left_basis = lax.dot_general(left, diag, nt_dims, precision=HIGHEST, preferred_element_type=F32)
    b_hi = left_basis.astype(BF16).astype(F32)
    b_lo = left_basis - b_hi
    wide = lax.broadcasted_iota(jnp.int32, (GROUP_ROWS, 128), 1)
    for j in range(GROUPS):
        n = GROUP_ROWS if j < GROUPS - 1 else HALF
        first = pltpu.roll(b_hi[:n], (128 - RANK * j) % 128, 1) if j else b_hi[:n]
        second = pltpu.roll(b_lo[:n], (128 + RANK - RANK * j) % 128, 1) if j != 1 else b_lo[:n]
        third = pltpu.roll(b_hi[:n], (128 + 2 * RANK - RANK * j) % 128, 1) if j != 2 else b_hi[:n]
        mixed = jnp.where(wide[:n] < RANK, first, jnp.where(wide[:n] < 2 * RANK, second, third))
        mixed = jnp.where(wide[:n] < 3 * RANK, mixed, 0.0)
        lhs_ref[GROUP_ROWS * j : GROUP_ROWS * j + n] = mixed.astype(BF16)
    i_hi, i_mid, i_lo = split3(inv[:, :RANK])
    inv_lhs = jnp.concatenate([i_hi, i_hi, i_mid, i_hi, i_mid, i_lo], axis=1)

    @on_core1()
    def _():
        arrived(rfull.at[:, pl.ds(0, NY - 1)], fr)

    @on_core0()
    def _():
        arrived(rfull, fr)

    rt = jnp.concatenate(
        [jnp.concatenate([rfull[h % 2, 2 * q + h // 2] for h in range(4)], axis=1) for q in range(RANK // 8)],
        axis=0,
    )
    r_hi, r_mid, r_lo = split3(rt)
    basis_t = jnp.dot(
        inv_lhs, jnp.concatenate([r_hi, r_mid, r_hi, r_lo, r_mid, r_hi], axis=0), preferred_element_type=F32
    )
    nb_ref[...] = basis_t

    @on_core0()
    def _():
        left_here(part, send_sem.at[0])
        left_here(rpart, send_sem.at[3])

    @on_core1()
    def _():
        left_here(part.at[:, pl.ds(0, NX - 1)], send_sem.at[0])
        left_here(xbuf, send_sem.at[1])
        left_here(xbuf, send_sem.at[2])
        left_here(rbuf1, send_sem.at[3])
        left_here(gbuf.at[pl.ds(0, NZ - 1)], send_sem.at[4])
        left_here(zbuf.at[:, pl.ds(0, NZ - 1)], send_sem.at[5])
        left_here(gsum, send_sem.at[6])
        left_here(rbuf0, send_sem.at[7])
        left_here(rbuf1, send_sem.at[8])


def update_kernel(gv, ev, lhs_ref, basis_ref, err_hbm, nb_hbm, out, sem):
    blocks = ROWS // HALF
    stores = [pltpu.make_async_copy(basis_ref, nb_hbm, sem.at[blocks])]
    stores[0].start()
    n_hi, n_lo = split2(basis_ref[...])
    rhs = jnp.concatenate([n_hi, n_hi, n_lo, jnp.zeros_like(n_lo)], axis=0)
    for b in range(blocks):
        sl = slice(HALF * b, HALF * (b + 1))
        rebuilt = jnp.dot(lhs_ref[sl, :], rhs, preferred_element_type=F32)
        merged = gv[sl, :].astype(F32) + ev[sl, :].astype(F32)
        out[sl, :] = (merged - rebuilt).astype(BF16)
        rows = pl.ds(HALF * b, HALF)
        copy = pltpu.make_async_copy(out.at[rows], err_hbm.at[rows], sem.at[b])
        copy.start()
        stores.append(copy)
    for copy in stores:
        copy.wait()


def on_device(gradients, error_buffer, warm_basis):
    vmem = pl.BlockSpec(memory_space=pltpu.VMEM)
    anyspace = pl.BlockSpec(memory_space=pl.ANY)
    dma = pltpu.SemaphoreType.DMA
    wide = (ROWS, COLS)
    kept = pl.pallas_call(
        factors_kernel,
        name="factors",
        out_shape=(
            pltpu.VMEM(wide, BF16),
            pltpu.VMEM(wide, BF16),
            pltpu.VMEM((ROWS, 128), BF16),
            pltpu.VMEM((RANK, COLS), F32),
        ),
        in_specs=[anyspace, anyspace, anyspace],
        out_specs=(vmem, vmem, vmem, vmem),
        scratch_shapes=[
            pltpu.VMEM((RANK, COLS), F32),
            pltpu.VMEM((CHUNKS, NX, PIECE, 128), F32),
            pltpu.VMEM((CHUNKS, 2 * NX - 1, PIECE, 128), F32),
            pltpu.VMEM((CHUNKS, NY, PIECE, 128), F32),
            pltpu.VMEM((CHUNKS, NX, PIECE, 128), F32),
            pltpu.VMEM((RCHUNKS, NY, 8, 128), F32),
            pltpu.VMEM((RCHUNKS, NY, 8, 128), F32),
            pltpu.VMEM((RCHUNKS, NY - 1, 8, 128), F32),
            pltpu.VMEM((RCHUNKS, NZ, 2, 8, 128), F32),
            pltpu.VMEM((RCHUNKS, 8, 128), F32),
            pltpu.VMEM((NZ, 8, 128), F32),
            pltpu.VMEM((8, 128), F32),
            pltpu.VMEM((RCHUNKS, NY, 8, 128), F32),
            dma((2 * GROUPS + 1,)),
            dma((9,)),
            dma((CHUNKS,)), dma((CHUNKS,)), dma((CHUNKS,)),
            dma, dma, dma((RCHUNKS,)), dma((RCHUNKS,)), dma((RCHUNKS,)), dma,
            pltpu.SemaphoreType.REGULAR((3,)),
        ],
        compiler_params=pltpu.CompilerParams(
            collective_id=0, has_side_effects=True, vmem_limit_bytes=24 * 1024 * 1024
        ),
    )(*(pltpu.with_memory_space_constraint(x, pltpu.HBM) for x in (gradients[0], error_buffer[0], warm_basis.T)))
    new_errors, basis_t = pl.pallas_call(
        update_kernel,
        name="update",
        out_shape=(jax.ShapeDtypeStruct(wide, BF16), jax.ShapeDtypeStruct((RANK, COLS), F32)),
        in_specs=[vmem, vmem, vmem, vmem],
        out_specs=(anyspace, anyspace),
        scratch_shapes=[pltpu.VMEM(wide, BF16), dma((ROWS // HALF + 1,))],
        compiler_params=pltpu.CompilerParams(vmem_limit_bytes=24 * 1024 * 1024),
    )(*(pltpu.with_memory_space_constraint(x, pltpu.VMEM) for x in kept))
    return new_errors[None], basis_t.T


def solution(mesh):
    placed = (P("dp", None, "tensor"), P("dp", None, "tensor"), P("tensor", None))
    return jax.shard_map(
        on_device,
        mesh=mesh,
        in_specs=placed,
        out_specs=(P("dp", None, "tensor"), P("tensor", None)),
        check_vma=False,
    )
```

time: 53 us -> 49.2 us (0.928)
  Pallas kernels: 51.8 us -> 48.4 us
    pallas_call x1, Pallas kernels: 50.5 us -> 47.1 us  [on_device(): pl.pallas_call(factors_kernel, name='factors', out_shape=(pltpu.VMEM(wide...]
where the time goes in v3:
time: 49.2 us; the launch traced here: 49.1 us
  Pallas kernels  48.4 us (98%)
  between operations  0.64 us (1%)
    pallas_call x1, Pallas kernels, on_device(): pl.pallas_call(factors_kernel, name='factors', out_shape=(pltpu.VMEM(wide...  47.1 us
    pallas_call x1, Pallas kernels, on_device(): pl.pallas_call(update_kernel, name='update', out_shape=(jax.ShapeDtypeStr...  1.33 us

profile of v3, /device:TPU:1, one launch (start us, length us, event | category | flops | bytes accessed | tf_op | source)
XLA Modules:
  0.0 49.1 jit_solution(5166080867574883943)
XLA Ops:
  0.6 47.1 %factors.1 = (bf16[1344,512]{1,0:T(8,128)(2,1)S(1)}, bf16[1344,512]{1,0:T(8,128)(2,1)S(1)}, bf16[1344,128]{1,0:T(8,128)(2,1)S(1)}, f32[32,512]{1,0:T(8,128)S(1)}) custom-call(bf16[1344,512]{1,0:T(8,128)(2,1)} %bitcast.5, bf16[1344,512]{1,0:T(8,128)(2,1)} %bitcast.6, f32[32,512]{1,0:T(8,128)} %bitcast.7), custom_call_target="tpu_custom_call" | custom-call | tf_op jit(solution)/shard_map/factors/pallas_call | solution.py:401
  47.7 1.3 %update.1 = (bf16[1344,512]{1,0:T(8,128)(2,1)}, f32[32,512]{1,0:T(8,128)}) custom-call(bf16[1344,512]{1,0:T(8,128)(2,1)S(1)} %get-tuple-element.8.gv, bf16[1344,512]{1,0:T(8,128)(2,1)S(1)} %get-tuple-element.9.ev, bf16[1344,128]{1,0:T(8,128)(2,1)S(1)} %get-tuple-element.10.lhs_ref, f32[32,512]{1,0:T(8,128)S(1)} %get-tuple-element.11.basis_ref), custom_call_target="tpu_custom_call" | custom-call | tf_op jit(solution)/shard_map/update/pallas_call | solution.py:436

commit v4 on v3

v4 whole, which is shorter than its diff:
```python
import functools

import jax
import jax.numpy as jnp
from jax import lax
from jax.experimental import pallas as pl
from jax.experimental.pallas import tpu as pltpu
from jax.sharding import PartitionSpec as P

MESH = pl.DeviceIdType.MESH
HIGHEST = lax.Precision.HIGHEST
F32 = jnp.float32
BF16 = jnp.bfloat16

NY = 8
NZ = 12
NX = 4
ROWS = 1344
COLS = 512
RANK = 32
GROUPS = 4
GROUP_ROWS = ROWS // GROUPS
BLOCK = 192
CHUNKS = ((0, 64, 64), (64, 96, 96), (160, 128, 128), (288, 48, 64))
PACKED = sum(padded for _, _, padded in CHUNKS)
RCHUNKS = 2

FIRST = 3
ORDER4 = (2, 1, 3)
ORDER8 = (4, 3, 5, 2, 6, 1, 7)


def pad_rows(block, rows):
    if block.shape[0] == rows:
        return block
    return jnp.concatenate([block, jnp.zeros((rows - block.shape[0], block.shape[1]), block.dtype)], axis=0)


def split2(x):
    hi = x.astype(BF16)
    return hi, (x - hi.astype(F32)).astype(BF16)


def split3(x):
    hi = x.astype(BF16)
    rest = x - hi.astype(F32)
    mid = rest.astype(BF16)
    return hi, mid, (rest - mid.astype(F32)).astype(BF16)


def inverse_lower(gram):
    lane = lax.broadcasted_iota(jnp.int32, (RANK, 128), 1)
    row = lax.broadcasted_iota(jnp.int32, (RANK, 128), 0)
    a = jnp.where(lane < RANK, gram, jnp.where(lane == row + RANK, 1.0, 0.0))
    for k in range(RANK - 1):
        pivot = a[k : k + 1, :]
        factor = a[:, k : k + 1] * (1.0 / pivot[:, k : k + 1])
        factor = jnp.where(row[:, :1] > k, factor, 0.0)
        a = a - factor * pivot
    diagonal = jnp.sum(jnp.where(lane == row, a, 0.0), axis=1, keepdims=True)
    inv = a * lax.rsqrt(diagonal)
    inv = jnp.where((lane >= RANK) & (lane < 2 * RANK), inv, 0.0)
    inv = inv + pltpu.roll(inv, 2 * RANK, 1)
    return inv + pltpu.roll(inv, RANK, 1)


def factors_kernel(
    g_hbm, e_hbm, wt_hbm, merged, lhs_ref, nb_ref,
    gv, ev, wt, wall, part, xbuf, ybuf, pfull, rpart, rbuf0, rbuf1, zbuf, zsum, gbuf, gsum, rfull, sizes,
    load_sem, send_sem, xr, yr, pr, gr, gm, rr0, rr1, zr, fr, reach_y, reach_z,
):
    dp = lax.axis_index("dp")
    t = lax.axis_index("tensor")
    y = lax.div(dp, NZ)
    z = lax.rem(dp, NZ)
    x = lax.div(t, 2)
    core = lax.rem(t, 2)

    def x_peer(k, c):
        return {"dp": dp, "tensor": lax.rem(x + k, NX) * 2 + c}

    def y_peer(k, c):
        return {"dp": lax.rem(y + k, NY) * NZ + z, "tensor": x * 2 + c}

    def z_peer(k):
        return {"dp": y * NZ + lax.rem(z + k, NZ), "tensor": t}

    z_peers = [{"dp": y * NZ + i + lax.div(i + NZ - z, NZ), "tensor": t} for i in range(NZ - 1)]

    def send(src, dst, ssem, rsem, peer):
        pltpu.make_async_remote_copy(
            src_ref=src, dst_ref=dst, send_sem=ssem, recv_sem=rsem, device_id=peer, device_id_type=MESH
        ).start()

    def arrived(ref, sem):
        pltpu.make_async_remote_copy(
            src_ref=ref, dst_ref=ref, send_sem=send_sem.at[0], recv_sem=sem, device_id=x_peer(1, core), device_id_type=MESH
        ).wait_recv()

    def left_here(ref, sem):
        pltpu.make_async_remote_copy(
            src_ref=ref, dst_ref=ref, send_sem=sem, recv_sem=xr.at[0], device_id=x_peer(1, core), device_id_type=MESH
        ).wait_send()

    def signal(sem, peer):
        pl.semaphore_signal(sem, inc=1, device_id=peer, device_id_type=MESH)

    on_core0 = functools.partial(pl.when, core == 0)
    on_core1 = functools.partial(pl.when, core == 1)

    wt_load = pltpu.make_async_copy(wt_hbm, wt, load_sem.at[2 * len(CHUNKS)])
    wt_load.start()

    def load(c):
        rows = pl.ds(*CHUNKS[c][:2])
        return [
            pltpu.make_async_copy(hbm.at[:, rows], ref.at[:, rows], load_sem.at[2 * c + i])
            for i, (hbm, ref) in enumerate(((g_hbm, gv), (e_hbm, ev)))
        ]

    loads = [load(c) for c in range(len(CHUNKS))]
    for copy in loads[0]:
        copy.start()

    barrier = pltpu.get_barrier_semaphore()

    @on_core1()
    def _():
        for k in ORDER4:
            signal(barrier, x_peer(k, 1))
            signal(barrier, x_peer(k, 0))
        for k in (1, NY - 1):
            signal(barrier, y_peer(k, 1))
        for k in (1, NZ - 1):
            signal(barrier, z_peer(k))
        signal(barrier, x_peer(0, 0))

    @on_core0()
    def _():
        for k in ORDER4 + (0,):
            signal(barrier, x_peer(k, 1))

    for copy in loads[1]:
        copy.start()

    wt_load.wait()
    for copy in loads[2] + loads[3]:
        copy.start()
    w_wide = jnp.concatenate([wt[...] * (1.0 / NY)] * GROUPS, axis=0).T
    group = lax.div(lax.broadcasted_iota(jnp.int32, (COLS, 128), 1), RANK)
    for j in range(GROUPS):
        banded = jnp.where(group == j, w_wide, 0.0)
        wall[COLS * j : COLS * (j + 1), :] = jnp.concatenate(split2(banded), axis=1)
    for c, (first, length, padded) in enumerate(CHUNKS):
        for copy in loads[c]:
            copy.wait()
        halves = [
            pad_rows(jnp.concatenate([ref[j, first : first + length, :] for j in range(GROUPS)], axis=1), padded)
            for ref in (gv, ev)
        ]
        acc = jnp.dot(jnp.concatenate(halves, axis=0), wall[...], preferred_element_type=F32)
        acc = acc[:padded] + acc[padded:]
        packed = acc[:, :128] + acc[:, 128:]
        piece = padded // NX
        for i in range(NX):
            part[c, i, :piece] = packed[piece * i : piece * (i + 1)]
        rows = pl.ds(0, piece)
        if c == 0:

            @on_core1()
            def _():
                pl.semaphore_wait(barrier, 2 * (NX - 1) + 1 + 2 + 2)
                for k in (1, NY - 1):
                    signal(reach_y.at[0], y_peer(k, 1))
                for k in (1, NZ - 1):
                    signal(reach_z.at[0], z_peer(k))

            @on_core0()
            def _():
                pl.semaphore_wait(barrier, NX)

        @on_core1()
        def _():
            for k in ORDER4:
                send(part.at[c, lax.rem(x + k, NX), rows], xbuf.at[c, k - 1, rows], send_sem.at[0], xr.at[c], x_peer(k, 1))

        @on_core0()
        def _():
            for k in ORDER4 + (0,):
                send(part.at[c, lax.rem(x + k, NX), rows], xbuf.at[c, NX - 1 + k, rows], send_sem.at[0], xr.at[c], x_peer(k, 1))

    @on_core1()
    def _():
        pl.semaphore_wait(reach_y.at[0], 2)
        for k in (2, NY - 2):
            signal(reach_y.at[1], y_peer(k, 1))
        for c, (_, _, padded) in enumerate(CHUNKS):
            rows = pl.ds(0, padded // NX)
            arrived(xbuf.at[c, :, rows], xr.at[c])
            if c == 0:
                pl.semaphore_wait(reach_y.at[1], 2)
            total = part[c, x, rows]
            for i in range(2 * NX - 1):
                total = total + xbuf[c, i, rows]
            ybuf[c, y, rows] = total
            for k in ORDER8:
                send(ybuf.at[c, y, rows], ybuf.at[c, y, rows], send_sem.at[1], yr.at[c], y_peer(k, 1))
        pl.semaphore_wait(reach_z.at[0], 2)
        for k in (2, NZ - 2):
            signal(reach_z.at[1], z_peer(k))
        for c, (_, _, padded) in enumerate(CHUNKS):
            if c == 1:
                pl.semaphore_wait(reach_z.at[1], 2)
                for k in (2, NZ - 2):
                    signal(reach_z.at[2], z_peer(k))
            rows = pl.ds(0, padded // NX)
            arrived(ybuf.at[c, pl.ds(0, NY - 1), rows], yr.at[c])
            total = ybuf[c, 0, rows]
            for i in range(1, NY):
                total = total + ybuf[c, i, rows]
            pfull[c, x, rows] = total
            for k in ORDER4:
                send(pfull.at[c, x, rows], pfull.at[c, x, rows], send_sem.at[2], pr.at[c], x_peer(k, 0))
                send(pfull.at[c, x, rows], pfull.at[c, x, rows], send_sem.at[2], pr.at[c], x_peer(k, 1))
            send(pfull.at[c, x, rows], pfull.at[c, x, rows], send_sem.at[2], pr.at[c], x_peer(0, 0))

    right = None
    bands = []
    for c, (first, length, padded) in enumerate(CHUNKS):
        rows = pl.ds(0, padded // NX)

        @on_core1()
        def _():
            arrived(pfull.at[c, pl.ds(0, NX - 1), rows], pr.at[c])

        @on_core0()
        def _():
            arrived(pfull.at[c, :, rows], pr.at[c])

        bands.append(jnp.concatenate([pfull[c, i, rows] for i in range(NX)], axis=0)[:length])
        left_t = pad_rows(bands[-1], 128).T
        lt = [left_t[RANK * j : RANK * (j + 1)] for j in range(GROUPS)]
        depth = 128
        if length <= 64:
            depth = 64
            lt = [lt[j] + pltpu.roll(lt[j + 1], 64, 1) for j in range(0, GROUPS, 2)]
        lt = jnp.concatenate(lt, axis=1)
        lhs = jnp.concatenate(split3(lt * (1.0 / NY)), axis=0)
        for ref in (gv, ev):
            block = jnp.concatenate(
                [pad_rows(ref[j, first : first + length, :], depth) for j in range(GROUPS)], axis=0
            )
            term = jnp.dot(lhs, block, preferred_element_type=F32)
            right = term if right is None else right + term
    right = right[:RANK] + (right[RANK : 2 * RANK] + right[2 * RANK :])
    for c in range(RCHUNKS):
        for i in range(NY):
            q, h = i // 2, 2 * (i % 2) + c
            rpart[c, i] = right[8 * q : 8 * q + 8, 128 * h : 128 * (h + 1)]
    left = jnp.concatenate(bands, axis=0)

    @on_core0()
    def _():
        for c in range(RCHUNKS):
            for k in ORDER8 + (0,):
                send(rpart.at[c, lax.rem(y + k, NY)], rbuf0.at[c, k], send_sem.at[3], rr0.at[c], y_peer(k, 1))
        arrived(gsum, gm)

    @on_core1()
    def _():
        for c in range(RCHUNKS):
            for k in ORDER8:
                send(rpart.at[c, lax.rem(y + k, NY)], rbuf1.at[c, k - 1], send_sem.at[3], rr1.at[c], y_peer(k, 1))

        blocks = jnp.dot(left.T, left, precision=HIGHEST, preferred_element_type=F32)
        lane8 = lax.broadcasted_iota(jnp.int32, (8, 128), 1)
        tile = jnp.zeros((8, 128), F32)
        for q in range(RANK // 8):
            rows8 = None
            for j in range(GROUPS):
                band = blocks[RANK * j + 8 * q : RANK * j + 8 * q + 8, :]
                band = jnp.where(lax.div(lane8, RANK) == j, band, 0.0)
                rows8 = band if rows8 is None else rows8 + band
            rows8 = rows8 + pltpu.roll(rows8, 64, 1)
            rows8 = rows8 + pltpu.roll(rows8, 32, 1)
            tile = jnp.where(lax.div(lane8, RANK) == q, rows8, tile)
        gbuf[z] = tile
        pl.semaphore_wait(reach_z.at[2], 2)
        for peer in z_peers:
            send(gbuf.at[z], gbuf.at[z], send_sem.at[4], gr, peer)

        for c in range(RCHUNKS):
            arrived(rbuf1.at[c], rr1.at[c])
            total = rpart[c, y]
            for i in range(NY - 1):
                total = total + rbuf1[c, i]
            zbuf[c, z, 1] = total
            arrived(rbuf0.at[c], rr0.at[c])
            total = rbuf0[c, 0]
            for i in range(1, NY):
                total = total + rbuf0[c, i]
            zbuf[c, z, 0] = total
            for peer in z_peers[:FIRST]:
                send(zbuf.at[c, z], zbuf.at[c, z], send_sem.at[5], zr.at[c], peer)
        for peer in z_peers[FIRST:]:
            for c in range(RCHUNKS):
                send(zbuf.at[c, z], zbuf.at[c, z], send_sem.at[5], zr.at[c], peer)

        arrived(gbuf.at[pl.ds(0, NZ - 1)], gr)
        tile = gbuf[0]
        for i in range(1, NZ):
            tile = tile + gbuf[i]
        gsum[...] = tile
        send(gsum, gsum, send_sem.at[6], gm, x_peer(0, 0))

    tile = gsum[...]
    rows = [tile] + [pltpu.roll(tile, 128 - 32 * q, 1) for q in range(1, RANK // 8)]
    inv = inverse_lower(jnp.concatenate(rows, axis=0))

    @on_core1()
    def _():
        for c in range(RCHUNKS):
            arrived(zbuf.at[c, pl.ds(0, NZ - 1)], zr.at[c])
            total = zbuf[c, 0]
            for i in range(1, NZ):
                total = total + zbuf[c, i]
            zsum[c] = total[0]
            rfull[c, y] = total[1]
            for k in ORDER8:
                send(zsum.at[c], rfull.at[c, y], send_sem.at[7], fr, y_peer(k, 0))
                send(rfull.at[c, y], rfull.at[c, y], send_sem.at[8], fr, y_peer(k, 1))
            send(zsum.at[c], rfull.at[c, y], send_sem.at[7], fr, x_peer(0, 0))

    lane = lax.broadcasted_iota(jnp.int32, (RANK, 128), 1)
    diag = jnp.concatenate(
        [jnp.where(lax.div(lane, RANK) == j, inv, 0.0) for j in range(GROUPS)], axis=0
    )
    left_basis = lax.dot_general(left, diag, (((1,), (1,)), ((), ())), precision=HIGHEST, preferred_element_type=F32)
    b_hi = left_basis.astype(BF16).astype(F32)
    b_lo = left_basis - b_hi
    wide = lax.broadcasted_iota(jnp.int32, (GROUP_ROWS, 128), 1)
    for j in range(GROUPS):
        first = pltpu.roll(b_hi, (128 - RANK * j) % 128, 1) if j else b_hi
        second = pltpu.roll(b_lo, (128 + RANK - RANK * j) % 128, 1) if j != 1 else b_lo
        third = pltpu.roll(b_hi, (128 + 2 * RANK - RANK * j) % 128, 1) if j != 2 else b_hi
        mixed = jnp.where(wide < RANK, first, jnp.where(wide < 2 * RANK, second, third))
        mixed = jnp.where(wide < 3 * RANK, mixed, 0.0)
        lhs_ref[GROUP_ROWS * j : GROUP_ROWS * (j + 1)] = mixed.astype(BF16)
        merged[GROUP_ROWS * j : GROUP_ROWS * (j + 1)] = gv[j].astype(F32) + ev[j].astype(F32)
    i_hi, i_mid, i_lo = split3(inv[:, :RANK])
    inv_lhs = jnp.concatenate([i_hi, i_hi, i_mid, i_hi, i_mid, i_lo], axis=1)

    @on_core1()
    def _():
        arrived(rfull.at[:, pl.ds(0, NY - 1)], fr)

    @on_core0()
    def _():
        arrived(rfull, fr)

    rt = jnp.concatenate(
        [jnp.concatenate([rfull[h % 2, 2 * q + h // 2] for h in range(4)], axis=1) for q in range(RANK // 8)],
        axis=0,
    )
    r_hi, r_mid, r_lo = split3(rt)
    basis_t = jnp.dot(
        inv_lhs, jnp.concatenate([r_hi, r_mid, r_hi, r_lo, r_mid, r_hi], axis=0), preferred_element_type=F32
    )
    nb_ref[...] = basis_t

    packed_piece = pl.ds(0, PACKED // NX)

    @on_core0()
    def _():
        left_here(sizes.at[pl.ds(0, NX), packed_piece], send_sem.at[0])
        left_here(rpart, send_sem.at[3])

    @on_core1()
    def _():
        left_here(sizes.at[pl.ds(0, NX - 1), packed_piece], send_sem.at[0])
        left_here(sizes.at[pl.ds(0, NY - 1), packed_piece], send_sem.at[1])
        left_here(sizes.at[pl.ds(0, 2 * NX - 1), packed_piece], send_sem.at[2])
        left_here(rbuf1, send_sem.at[3])
        left_here(gbuf.at[pl.ds(0, NZ - 1)], send_sem.at[4])
        left_here(zbuf.at[:, pl.ds(0, NZ - 1)], send_sem.at[5])
        left_here(gsum, send_sem.at[6])
        left_here(rbuf0, send_sem.at[7])
        left_here(rbuf1, send_sem.at[8])


def update_kernel(merged, lhs_ref, basis_ref, err_hbm, nb_hbm, out, sem):
    blocks = ROWS // BLOCK
    stores = [pltpu.make_async_copy(basis_ref, nb_hbm, sem.at[blocks])]
    stores[0].start()
    n_hi, n_lo = split2(basis_ref[...])
    rhs = jnp.concatenate([n_hi, n_hi, n_lo, jnp.zeros_like(n_lo)], axis=0)
    for b in range(blocks):
        sl = slice(BLOCK * b, BLOCK * (b + 1))
        rebuilt = jnp.dot(lhs_ref[sl, :], rhs, preferred_element_type=F32)
        out[sl, :] = (merged[sl, :] - rebuilt).astype(BF16)
        rows = pl.ds(BLOCK * b, BLOCK)
        copy = pltpu.make_async_copy(out.at[rows], err_hbm.at[rows], sem.at[b])
        copy.start()
        stores.append(copy)
    for copy in stores:
        copy.wait()


def on_device(gradients, error_buffer, warm_basis):
    vmem = pl.BlockSpec(memory_space=pltpu.VMEM)
    anyspace = pl.BlockSpec(memory_space=pl.ANY)
    dma = pltpu.SemaphoreType.DMA
    wide = (ROWS, COLS)
    grouped = (GROUPS, GROUP_ROWS, COLS)
    nc, piece = len(CHUNKS), max(padded for _, _, padded in CHUNKS) // NX
    inputs = (gradients.reshape(grouped), error_buffer.reshape(grouped), warm_basis.T)
    kept = pl.pallas_call(
        factors_kernel,
        name="factors",
        out_shape=(
            pltpu.VMEM(wide, F32),
            pltpu.VMEM((ROWS, 128), BF16),
            pltpu.VMEM((RANK, COLS), F32),
        ),
        in_specs=[anyspace, anyspace, anyspace],
        out_specs=(vmem, vmem, vmem),
        scratch_shapes=[
            pltpu.VMEM(grouped, BF16),
            pltpu.VMEM(grouped, BF16),
            pltpu.VMEM((RANK, COLS), F32),
            pltpu.VMEM((GROUPS * COLS, 256), BF16),
            pltpu.VMEM((nc, NX, piece, 128), F32),
            pltpu.VMEM((nc, 2 * NX - 1, piece, 128), F32),
            pltpu.VMEM((nc, NY, piece, 128), F32),
            pltpu.VMEM((nc, NX, piece, 128), F32),
            pltpu.VMEM((RCHUNKS, NY, 8, 128), F32),
            pltpu.VMEM((RCHUNKS, NY, 8, 128), F32),
            pltpu.VMEM((RCHUNKS, NY - 1, 8, 128), F32),
            pltpu.VMEM((RCHUNKS, NZ, 2, 8, 128), F32),
            pltpu.VMEM((RCHUNKS, 8, 128), F32),
            pltpu.VMEM((NZ, 8, 128), F32),
            pltpu.VMEM((8, 128), F32),
            pltpu.VMEM((RCHUNKS, NY, 8, 128), F32),
            pltpu.VMEM((NY, PACKED // NX, 128), F32),
            dma((2 * nc + 1,)),
            dma((9,)),
            dma((nc,)), dma((nc,)), dma((nc,)),
            dma, dma, dma((RCHUNKS,)), dma((RCHUNKS,)), dma((RCHUNKS,)), dma,
            pltpu.SemaphoreType.REGULAR((2,)), pltpu.SemaphoreType.REGULAR((3,)),
        ],
        compiler_params=pltpu.CompilerParams(
            collective_id=0, has_side_effects=True, vmem_limit_bytes=24 * 1024 * 1024
        ),
    )(*(pltpu.with_memory_space_constraint(x, pltpu.HBM) for x in inputs))
    new_errors, basis_t = pl.pallas_call(
        update_kernel,
        name="update",
        out_shape=(jax.ShapeDtypeStruct(wide, BF16), jax.ShapeDtypeStruct((RANK, COLS), F32)),
        in_specs=[vmem, vmem, vmem],
        out_specs=(anyspace, anyspace),
        scratch_shapes=[pltpu.VMEM(wide, BF16), dma((ROWS // BLOCK + 1,))],
        compiler_params=pltpu.CompilerParams(vmem_limit_bytes=24 * 1024 * 1024),
    )(*(pltpu.with_memory_space_constraint(x, pltpu.VMEM) for x in kept))
    return new_errors[None], basis_t.T


def solution(mesh):
    placed = (P("dp", None, "tensor"), P("dp", None, "tensor"), P("tensor", None))
    return jax.shard_map(
        on_device,
        mesh=mesh,
        in_specs=placed,
        out_specs=(P("dp", None, "tensor"), P("tensor", None)),
        check_vma=False,
    )
```

time: 49.2 us -> 47.5 us (0.965)
  Pallas kernels: 48.4 us -> 46.7 us
    pallas_call x1, Pallas kernels: 47.1 us -> 45.4 us  [on_device(): pl.pallas_call(factors_kernel, name='factors', out_shape=(pltpu.VMEM(wide...]
where the time goes in v4:
time: 47.5 us; the launch traced here: 47.3 us
  Pallas kernels  46.7 us (98%)
  between operations  0.64 us (1%)
    pallas_call x1, Pallas kernels, on_device(): pl.pallas_call(factors_kernel, name='factors', out_shape=(pltpu.VMEM(wide...  45.4 us
    pallas_call x1, Pallas kernels, on_device(): pl.pallas_call(update_kernel, name='update', out_shape=(jax.ShapeDtypeStr...  1.33 us

profile of v4, /device:TPU:1, one launch (start us, length us, event | category | flops | bytes accessed | tf_op | source)
XLA Modules:
  0.0 47.3 jit_solution(13618916646065377526)
XLA Ops:
  0.6 45.4 %factors.1 = (f32[1344,512]{1,0:T(8,128)S(1)}, bf16[1344,128]{1,0:T(8,128)(2,1)S(1)}, f32[32,512]{1,0:T(8,128)S(1)}) custom-call(bf16[4,336,512]{2,1,0:T(8,128)(2,1)} %bitcast.5, bf16[4,336,512]{2,1,0:T(8,128)(2,1)} %bitcast.6, f32[32,512]{1,0:T(8,128)} %bitcast.7), custom_call_target="tpu_custom_call" | custom-call | tf_op jit(solution)/shard_map/factors/pallas_call | solution.py:417
  46.0 1.3 %update.1 = (bf16[1344,512]{1,0:T(8,128)(2,1)}, f32[32,512]{1,0:T(8,128)}) custom-call(f32[1344,512]{1,0:T(8,128)S(1)} %get-tuple-element.7.merged, bf16[1344,128]{1,0:T(8,128)(2,1)S(1)} %get-tuple-element.8.lhs_ref, f32[32,512]{1,0:T(8,128)S(1)} %get-tuple-element.9.basis_ref), custom_call_target="tpu_custom_call" | custom-call | tf_op jit(solution)/shard_map/update/pallas_call | solution.py:455

commit v5 on v4

--- a/solution.py
+++ b/solution.py
@@ -25,7 +25,9 @@
 PACKED = sum(padded for _, _, padded in CHUNKS)
 RCHUNKS = 2
 
-FIRST = 3
+SENT0 = NX * PACKED // NX // 8 + RCHUNKS * NY
+SENT1 = (17 * PACKED // NX // 8) + RCHUNKS * 7 + 11 + RCHUNKS * 11 * 2 + 1 + RCHUNKS * 15
+FIRST = 1
 ORDER4 = (2, 1, 3)
 ORDER8 = (4, 3, 5, 2, 6, 1, 7)
 
@@ -66,8 +68,8 @@
 
 def factors_kernel(
     g_hbm, e_hbm, wt_hbm, merged, lhs_ref, nb_ref,
-    gv, ev, wt, wall, part, xbuf, ybuf, pfull, rpart, rbuf0, rbuf1, zbuf, zsum, gbuf, gsum, rfull, sizes,
-    load_sem, send_sem, xr, yr, pr, gr, gm, rr0, rr1, zr, fr, reach_y, reach_z,
+    both, wt, wall, part, xbuf, ybuf, pfull, rpart, rbuf, zbuf, zsum, gbuf, gsum, rfull, sizes,
+    load_sem, send_sem, xr, yr, pr, gr, gm, rr, zr, fr, reach_y, reach_z,
 ):
     dp = lax.axis_index("dp")
     t = lax.axis_index("tensor")
@@ -94,7 +96,7 @@
 
     def arrived(ref, sem):
         pltpu.make_async_remote_copy(
-            src_ref=ref, dst_ref=ref, send_sem=send_sem.at[0], recv_sem=sem, device_id=x_peer(1, core), device_id_type=MESH
+            src_ref=ref, dst_ref=ref, send_sem=send_sem, recv_sem=sem, device_id=x_peer(1, core), device_id_type=MESH
         ).wait_recv()
 
     def left_here(ref, sem):
@@ -108,19 +110,15 @@
     on_core0 = functools.partial(pl.when, core == 0)
     on_core1 = functools.partial(pl.when, core == 1)
 
-    wt_load = pltpu.make_async_copy(wt_hbm, wt, load_sem.at[2 * len(CHUNKS)])
+    wt_load = pltpu.make_async_copy(wt_hbm, wt, load_sem.at[len(CHUNKS)])
     wt_load.start()
 
     def load(c):
         rows = pl.ds(*CHUNKS[c][:2])
-        return [
-            pltpu.make_async_copy(hbm.at[:, rows], ref.at[:, rows], load_sem.at[2 * c + i])
-            for i, (hbm, ref) in enumerate(((g_hbm, gv), (e_hbm, ev)))
-        ]
-
-    loads = [load(c) for c in range(len(CHUNKS))]
-    for copy in loads[0]:
-        copy.start()
+        for i, hbm in enumerate((g_hbm, e_hbm)):
+            pltpu.make_async_copy(hbm.at[:, rows], both.at[i, :, rows], load_sem.at[c]).start()
+
+    load(0)
 
     barrier = pltpu.get_barrier_semaphore()
 
@@ -140,23 +138,22 @@
         for k in ORDER4 + (0,):
             signal(barrier, x_peer(k, 1))
 
-    for copy in loads[1]:
-        copy.start()
+    load(1)
 
     wt_load.wait()
-    for copy in loads[2] + loads[3]:
-        copy.start()
+    load(2)
+    load(3)
     w_wide = jnp.concatenate([wt[...] * (1.0 / NY)] * GROUPS, axis=0).T
     group = lax.div(lax.broadcasted_iota(jnp.int32, (COLS, 128), 1), RANK)
     for j in range(GROUPS):
         banded = jnp.where(group == j, w_wide, 0.0)
         wall[COLS * j : COLS * (j + 1), :] = jnp.concatenate(split2(banded), axis=1)
     for c, (first, length, padded) in enumerate(CHUNKS):
-        for copy in loads[c]:
-            copy.wait()
+        rows = pl.ds(first, length)
+        pltpu.make_async_copy(both.at[:, :, rows], both.at[:, :, rows], load_sem.at[c]).wait()
         halves = [
-            pad_rows(jnp.concatenate([ref[j, first : first + length, :] for j in range(GROUPS)], axis=1), padded)
-            for ref in (gv, ev)
+            pad_rows(jnp.concatenate([both[i, j, first : first + length, :] for j in range(GROUPS)], axis=1), padded)
+            for i in range(2)
         ]
         acc = jnp.dot(jnp.concatenate(halves, axis=0), wall[...], preferred_element_type=F32)
         acc = acc[:padded] + acc[padded:]
@@ -182,12 +179,12 @@
         @on_core1()
         def _():
             for k in ORDER4:
-                send(part.at[c, lax.rem(x + k, NX), rows], xbuf.at[c, k - 1, rows], send_sem.at[0], xr.at[c], x_peer(k, 1))
+                send(part.at[c, lax.rem(x + k, NX), rows], xbuf.at[c, k - 1, rows], send_sem, xr.at[c], x_peer(k, 1))
 
         @on_core0()
         def _():
             for k in ORDER4 + (0,):
-                send(part.at[c, lax.rem(x + k, NX), rows], xbuf.at[c, NX - 1 + k, rows], send_sem.at[0], xr.at[c], x_peer(k, 1))
+                send(part.at[c, lax.rem(x + k, NX), rows], xbuf.at[c, NX - 1 + k, rows], send_sem, xr.at[c], x_peer(k, 1))
 
     @on_core1()
     def _():
@@ -204,7 +201,7 @@
                 total = total + xbuf[c, i, rows]
             ybuf[c, y, rows] = total
             for k in ORDER8:
-                send(ybuf.at[c, y, rows], ybuf.at[c, y, rows], send_sem.at[1], yr.at[c], y_peer(k, 1))
+                send(ybuf.at[c, y, rows], ybuf.at[c, y, rows], send_sem, yr.at[c], y_peer(k, 1))
         pl.semaphore_wait(reach_z.at[0], 2)
         for k in (2, NZ - 2):
             signal(reach_z.at[1], z_peer(k))
@@ -220,9 +217,9 @@
                 total = total + ybuf[c, i, rows]
             pfull[c, x, rows] = total
             for k in ORDER4:
-                send(pfull.at[c, x, rows], pfull.at[c, x, rows], send_sem.at[2], pr.at[c], x_peer(k, 0))
-                send(pfull.at[c, x, rows], pfull.at[c, x, rows], send_sem.at[2], pr.at[c], x_peer(k, 1))
-            send(pfull.at[c, x, rows], pfull.at[c, x, rows], send_sem.at[2], pr.at[c], x_peer(0, 0))
+                send(pfull.at[c, x, rows], pfull.at[c, x, rows], send_sem, pr.at[c], x_peer(k, 0))
+                send(pfull.at[c, x, rows], pfull.at[c, x, rows], send_sem, pr.at[c], x_peer(k, 1))
+            send(pfull.at[c, x, rows], pfull.at[c, x, rows], send_sem, pr.at[c], x_peer(0, 0))
 
     right = None
     bands = []
@@ -246,9 +243,9 @@
             lt = [lt[j] + pltpu.roll(lt[j + 1], 64, 1) for j in range(0, GROUPS, 2)]
         lt = jnp.concatenate(lt, axis=1)
         lhs = jnp.concatenate(split3(lt * (1.0 / NY)), axis=0)
-        for ref in (gv, ev):
+        for i in range(2):
             block = jnp.concatenate(
-                [pad_rows(ref[j, first : first + length, :], depth) for j in range(GROUPS)], axis=0
+                [pad_rows(both[i, j, first : first + length, :], depth) for j in range(GROUPS)], axis=0
             )
             term = jnp.dot(lhs, block, preferred_element_type=F32)
             right = term if right is None else right + term
@@ -263,14 +260,14 @@
     def _():
         for c in range(RCHUNKS):
             for k in ORDER8 + (0,):
-                send(rpart.at[c, lax.rem(y + k, NY)], rbuf0.at[c, k], send_sem.at[3], rr0.at[c], y_peer(k, 1))
+                send(rpart.at[c, lax.rem(y + k, NY)], rbuf.at[c, NY - 1 + k], send_sem, rr.at[c], y_peer(k, 1))
         arrived(gsum, gm)
 
     @on_core1()
     def _():
         for c in range(RCHUNKS):
             for k in ORDER8:
-                send(rpart.at[c, lax.rem(y + k, NY)], rbuf1.at[c, k - 1], send_sem.at[3], rr1.at[c], y_peer(k, 1))
+                send(rpart.at[c, lax.rem(y + k, NY)], rbuf.at[c, k - 1], send_sem, rr.at[c], y_peer(k, 1))
 
         blocks = jnp.dot(left.T, left, precision=HIGHEST, preferred_element_type=F32)
         lane8 = lax.broadcasted_iota(jnp.int32, (8, 128), 1)
@@ -287,31 +284,30 @@
         gbuf[z] = tile
         pl.semaphore_wait(reach_z.at[2], 2)
         for peer in z_peers:
-            send(gbuf.at[z], gbuf.at[z], send_sem.at[4], gr, peer)
+            send(gbuf.at[z], gbuf.at[z], send_sem, gr, peer)
 
         for c in range(RCHUNKS):
-            arrived(rbuf1.at[c], rr1.at[c])
+            arrived(rbuf.at[c], rr.at[c])
             total = rpart[c, y]
             for i in range(NY - 1):
-                total = total + rbuf1[c, i]
+                total = total + rbuf[c, i]
             zbuf[c, z, 1] = total
-            arrived(rbuf0.at[c], rr0.at[c])
-            total = rbuf0[c, 0]
-            for i in range(1, NY):
-                total = total + rbuf0[c, i]
+            total = rbuf[c, NY - 1]
+            for i in range(NY, 2 * NY - 1):
+                total = total + rbuf[c, i]
             zbuf[c, z, 0] = total
             for peer in z_peers[:FIRST]:
-                send(zbuf.at[c, z], zbuf.at[c, z], send_sem.at[5], zr.at[c], peer)
+                send(zbuf.at[c, z], zbuf.at[c, z], send_sem, zr.at[c], peer)
         for peer in z_peers[FIRST:]:
             for c in range(RCHUNKS):
-                send(zbuf.at[c, z], zbuf.at[c, z], send_sem.at[5], zr.at[c], peer)
+                send(zbuf.at[c, z], zbuf.at[c, z], send_sem, zr.at[c], peer)
 
         arrived(gbuf.at[pl.ds(0, NZ - 1)], gr)
         tile = gbuf[0]
         for i in range(1, NZ):
             tile = tile + gbuf[i]
         gsum[...] = tile
-        send(gsum, gsum, send_sem.at[6], gm, x_peer(0, 0))
+        send(gsum, gsum, send_sem, gm, x_peer(0, 0))
 
     tile = gsum[...]
     rows = [tile] + [pltpu.roll(tile, 128 - 32 * q, 1) for q in range(1, RANK // 8)]
@@ -327,9 +323,9 @@
             zsum[c] = total[0]
             rfull[c, y] = total[1]
             for k in ORDER8:
-                send(zsum.at[c], rfull.at[c, y], send_sem.at[7], fr, y_peer(k, 0))
-                send(rfull.at[c, y], rfull.at[c, y], send_sem.at[8], fr, y_peer(k, 1))
-            send(zsum.at[c], rfull.at[c, y], send_sem.at[7], fr, x_peer(0, 0))
+                send(zsum.at[c], rfull.at[c, y], send_sem, fr.at[c], y_peer(k, 0))
+                send(rfull.at[c, y], rfull.at[c, y], send_sem, fr.at[c], y_peer(k, 1))
+            send(zsum.at[c], rfull.at[c, y], send_sem, fr.at[c], x_peer(0, 0))
 
     lane = lax.broadcasted_iota(jnp.int32, (RANK, 128), 1)
     diag = jnp.concatenate(
@@ -346,46 +342,38 @@
         mixed = jnp.where(wide < RANK, first, jnp.where(wide < 2 * RANK, second, third))
         mixed = jnp.where(wide < 3 * RANK, mixed, 0.0)
         lhs_ref[GROUP_ROWS * j : GROUP_ROWS * (j + 1)] = mixed.astype(BF16)
-        merged[GROUP_ROWS * j : GROUP_ROWS * (j + 1)] = gv[j].astype(F32) + ev[j].astype(F32)
+        merged[GROUP_ROWS * j : GROUP_ROWS * (j + 1)] = both[0, j].astype(F32) + both[1, j].astype(F32)
     i_hi, i_mid, i_lo = split3(inv[:, :RANK])
     inv_lhs = jnp.concatenate([i_hi, i_hi, i_mid, i_hi, i_mid, i_lo], axis=1)
 
+    for c in range(RCHUNKS):
+
+        @on_core1()
+        def _():
+            arrived(rfull.at[c, pl.ds(0, NY - 1)], fr.at[c])
+
+        @on_core0()
+        def _():
+            arrived(rfull.at[c], fr.at[c])
+
+        rt = jnp.concatenate(
+            [jnp.concatenate([rfull[c, 2 * q], rfull[c, 2 * q + 1]], axis=1) for q in range(RANK // 8)], axis=0
+        )
+        r_hi, r_mid, r_lo = split3(rt)
+        basis_t = jnp.dot(
+            inv_lhs, jnp.concatenate([r_hi, r_mid, r_hi, r_lo, r_mid, r_hi], axis=0), preferred_element_type=F32
+        )
+        for h in range(2):
+            columns = slice(128 * (2 * h + c), 128 * (2 * h + c + 1))
+            nb_ref[:, columns] = basis_t[:, 128 * h : 128 * (h + 1)]
+
+    @on_core0()
+    def _():
+        left_here(sizes.at[pl.ds(0, SENT0)], send_sem)
+
     @on_core1()
     def _():
-        arrived(rfull.at[:, pl.ds(0, NY - 1)], fr)
-
-    @on_core0()
-    def _():
-        arrived(rfull, fr)
-
-    rt = jnp.concatenate(
-        [jnp.concatenate([rfull[h % 2, 2 * q + h // 2] for h in range(4)], axis=1) for q in range(RANK // 8)],
-        axis=0,
-    )
-    r_hi, r_mid, r_lo = split3(rt)
-    basis_t = jnp.dot(
-        inv_lhs, jnp.concatenate([r_hi, r_mid, r_hi, r_lo, r_mid, r_hi], axis=0), preferred_element_type=F32
-    )
-    nb_ref[...] = basis_t
-
-    packed_piece = pl.ds(0, PACKED // NX)
-
-    @on_core0()
-    def _():
-        left_here(sizes.at[pl.ds(0, NX), packed_piece], send_sem.at[0])
-        left_here(rpart, send_sem.at[3])
-
-    @on_core1()
-    def _():
-        left_here(sizes.at[pl.ds(0, NX - 1), packed_piece], send_sem.at[0])
-        left_here(sizes.at[pl.ds(0, NY - 1), packed_piece], send_sem.at[1])
-        left_here(sizes.at[pl.ds(0, 2 * NX - 1), packed_piece], send_sem.at[2])
-        left_here(rbuf1, send_sem.at[3])
-        left_here(gbuf.at[pl.ds(0, NZ - 1)], send_sem.at[4])
-        left_here(zbuf.at[:, pl.ds(0, NZ - 1)], send_sem.at[5])
-        left_here(gsum, send_sem.at[6])
-        left_here(rbuf0, send_sem.at[7])
-        left_here(rbuf1, send_sem.at[8])
+        left_here(sizes, send_sem)
 
 
 def update_kernel(merged, lhs_ref, basis_ref, err_hbm, nb_hbm, out, sem):
@@ -425,8 +413,7 @@
         in_specs=[anyspace, anyspace, anyspace],
         out_specs=(vmem, vmem, vmem),
         scratch_shapes=[
-            pltpu.VMEM(grouped, BF16),
-            pltpu.VMEM(grouped, BF16),
+            pltpu.VMEM((2,) + grouped, BF16),
             pltpu.VMEM((RANK, COLS), F32),
             pltpu.VMEM((GROUPS * COLS, 256), BF16),
             pltpu.VMEM((nc, NX, piece, 128), F32),
@@ -434,18 +421,17 @@
             pltpu.VMEM((nc, NY, piece, 128), F32),
             pltpu.VMEM((nc, NX, piece, 128), F32),
             pltpu.VMEM((RCHUNKS, NY, 8, 128), F32),
-            pltpu.VMEM((RCHUNKS, NY, 8, 128), F32),
-            pltpu.VMEM((RCHUNKS, NY - 1, 8, 128), F32),
+            pltpu.VMEM((RCHUNKS, 2 * NY - 1, 8, 128), F32),
             pltpu.VMEM((RCHUNKS, NZ, 2, 8, 128), F32),
             pltpu.VMEM((RCHUNKS, 8, 128), F32),
             pltpu.VMEM((NZ, 8, 128), F32),
             pltpu.VMEM((8, 128), F32),
             pltpu.VMEM((RCHUNKS, NY, 8, 128), F32),
-            pltpu.VMEM((NY, PACKED // NX, 128), F32),
-            dma((2 * nc + 1,)),
-            dma((9,)),
+            pltpu.VMEM((SENT1, 8, 128), F32),
+            dma((nc + 1,)),
+            dma,
             dma((nc,)), dma((nc,)), dma((nc,)),
-            dma, dma, dma((RCHUNKS,)), dma((RCHUNKS,)), dma((RCHUNKS,)), dma,
+            dma, dma, dma((RCHUNKS,)), dma((RCHUNKS,)), dma((RCHUNKS,)),
             pltpu.SemaphoreType.REGULAR((2,)), pltpu.SemaphoreType.REGULAR((3,)),
         ],
         compiler_params=pltpu.CompilerParams(

time: 47.5 us -> 47.3 us (level)
  no operation moved by 1% of the time
where the time goes in v5:
time: 47.3 us; the launch traced here: 47.1 us
  Pallas kernels  46.5 us (98%)
  between operations  0.64 us (1%)
    pallas_call x1, Pallas kernels, on_device(): pl.pallas_call(factors_kernel, name='factors', out_shape=(pltpu.VMEM(wide...  45.1 us
    pallas_call x1, Pallas kernels, on_device(): pl.pallas_call(update_kernel, name='update', out_shape=(jax.ShapeDtypeStr...  1.33 us

profile of v5, /device:TPU:1, one launch (start us, length us, event | category | flops | bytes accessed | tf_op | source)
XLA Modules:
  0.0 47.1 jit_solution(3086408955305616633)
XLA Ops:
  0.6 45.1 %factors.1 = (f32[1344,512]{1,0:T(8,128)S(1)}, bf16[1344,128]{1,0:T(8,128)(2,1)S(1)}, f32[32,512]{1,0:T(8,128)S(1)}) custom-call(bf16[4,336,512]{2,1,0:T(8,128)(2,1)} %bitcast.5, bf16[4,336,512]{2,1,0:T(8,128)(2,1)} %bitcast.6, f32[32,512]{1,0:T(8,128)} %bitcast.7), custom_call_target="tpu_custom_call" | custom-call | tf_op jit(solution)/shard_map/factors/pallas_call | solution.py:405
  45.8 1.3 %update.1 = (bf16[1344,512]{1,0:T(8,128)(2,1)}, f32[32,512]{1,0:T(8,128)}) custom-call(f32[1344,512]{1,0:T(8,128)S(1)} %get-tuple-element.7.merged, bf16[1344,128]{1,0:T(8,128)(2,1)S(1)} %get-tuple-element.8.lhs_ref, f32[32,512]{1,0:T(8,128)S(1)} %get-tuple-element.9.basis_ref), custom_call_target="tpu_custom_call" | custom-call | tf_op jit(solution)/shard_map/update/pallas_call | solution.py:441

commit v6 on v5

--- a/solution.py
+++ b/solution.py
@@ -21,7 +21,8 @@
 GROUPS = 4
 GROUP_ROWS = ROWS // GROUPS
 BLOCK = 192
-CHUNKS = ((0, 64, 64), (64, 96, 96), (160, 128, 128), (288, 48, 64))
+HALF = COLS // 2
+CHUNKS = ((0, 96, 96), (96, 128, 128), (224, 112, 128))
 PACKED = sum(padded for _, _, padded in CHUNKS)
 RCHUNKS = 2
 
@@ -66,8 +67,13 @@
     return inv + pltpu.roll(inv, RANK, 1)
 
 
+def update_rhs(basis_t):
+    hi, lo = split2(basis_t)
+    return jnp.concatenate([hi, hi, lo, jnp.zeros_like(lo)], axis=0)
+
+
 def factors_kernel(
-    g_hbm, e_hbm, wt_hbm, merged, lhs_ref, nb_ref,
+    g_hbm, e_hbm, wt_hbm, merged, lhs_ref, nb_ref, done,
     both, wt, wall, part, xbuf, ybuf, pfull, rpart, rbuf, zbuf, zsum, gbuf, gsum, rfull, sizes,
     load_sem, send_sem, xr, yr, pr, gr, gm, rr, zr, fr, reach_y, reach_z,
 ):
@@ -89,6 +95,9 @@
 
     z_peers = [{"dp": y * NZ + i + lax.div(i + NZ - z, NZ), "tensor": t} for i in range(NZ - 1)]
 
+    y_rows = [(i + lax.div(i + NY - y, NY)) * NZ + z for i in range(NY - 1)]
+    y_peers = [[{"dp": row, "tensor": x * 2 + c} for c in range(2)] for row in y_rows]
+
     def send(src, dst, ssem, rsem, peer):
         pltpu.make_async_remote_copy(
             src_ref=src, dst_ref=dst, send_sem=ssem, recv_sem=rsem, device_id=peer, device_id_type=MESH
@@ -142,7 +151,6 @@
 
     wt_load.wait()
     load(2)
-    load(3)
     w_wide = jnp.concatenate([wt[...] * (1.0 / NY)] * GROUPS, axis=0).T
     group = lax.div(lax.broadcasted_iota(jnp.int32, (COLS, 128), 1), RANK)
     for j in range(GROUPS):
@@ -252,7 +260,7 @@
     right = right[:RANK] + (right[RANK : 2 * RANK] + right[2 * RANK :])
     for c in range(RCHUNKS):
         for i in range(NY):
-            q, h = i // 2, 2 * (i % 2) + c
+            q, h = i // 2, 2 * c + i % 2
             rpart[c, i] = right[8 * q : 8 * q + 8, 128 * h : 128 * (h + 1)]
     left = jnp.concatenate(bands, axis=0)
 
@@ -322,9 +330,9 @@
                 total = total + zbuf[c, i]
             zsum[c] = total[0]
             rfull[c, y] = total[1]
-            for k in ORDER8:
-                send(zsum.at[c], rfull.at[c, y], send_sem, fr.at[c], y_peer(k, 0))
-                send(rfull.at[c, y], rfull.at[c, y], send_sem, fr.at[c], y_peer(k, 1))
+            for peer0, peer1 in y_peers:
+                send(rfull.at[c, y], rfull.at[c, y], send_sem, fr.at[c], peer1)
+                send(zsum.at[c], rfull.at[c, y], send_sem, fr.at[c], peer0)
             send(zsum.at[c], rfull.at[c, y], send_sem, fr.at[c], x_peer(0, 0))
 
     lane = lax.broadcasted_iota(jnp.int32, (RANK, 128), 1)
@@ -363,9 +371,13 @@
         basis_t = jnp.dot(
             inv_lhs, jnp.concatenate([r_hi, r_mid, r_hi, r_lo, r_mid, r_hi], axis=0), preferred_element_type=F32
         )
-        for h in range(2):
-            columns = slice(128 * (2 * h + c), 128 * (2 * h + c + 1))
-            nb_ref[:, columns] = basis_t[:, 128 * h : 128 * (h + 1)]
+        nb_ref[:, HALF * c : HALF * (c + 1)] = basis_t
+        if c == 0:
+            rhs = update_rhs(basis_t)
+            for b in range(ROWS // BLOCK):
+                rows = slice(BLOCK * b, BLOCK * (b + 1))
+                rebuilt = jnp.dot(lhs_ref[rows, :], rhs, preferred_element_type=F32)
+                done[rows, :] = (merged[rows, :HALF] - rebuilt).astype(BF16)
 
     @on_core0()
     def _():
@@ -376,18 +388,21 @@
         left_here(sizes, send_sem)
 
 
-def update_kernel(merged, lhs_ref, basis_ref, err_hbm, nb_hbm, out, sem):
+def update_kernel(merged, lhs_ref, basis_ref, done, err_hbm, nb_hbm, out, sem):
     blocks = ROWS // BLOCK
-    stores = [pltpu.make_async_copy(basis_ref, nb_hbm, sem.at[blocks])]
-    stores[0].start()
-    n_hi, n_lo = split2(basis_ref[...])
-    rhs = jnp.concatenate([n_hi, n_hi, n_lo, jnp.zeros_like(n_lo)], axis=0)
+    stores = [
+        pltpu.make_async_copy(done, err_hbm.at[:, pl.ds(0, HALF)], sem.at[blocks]),
+        pltpu.make_async_copy(basis_ref, nb_hbm, sem.at[blocks + 1]),
+    ]
+    for copy in stores:
+        copy.start()
+    rhs = update_rhs(basis_ref[:, HALF:])
     for b in range(blocks):
         sl = slice(BLOCK * b, BLOCK * (b + 1))
         rebuilt = jnp.dot(lhs_ref[sl, :], rhs, preferred_element_type=F32)
-        out[sl, :] = (merged[sl, :] - rebuilt).astype(BF16)
+        out[sl, :] = (merged[sl, HALF:] - rebuilt).astype(BF16)
         rows = pl.ds(BLOCK * b, BLOCK)
-        copy = pltpu.make_async_copy(out.at[rows], err_hbm.at[rows], sem.at[b])
+        copy = pltpu.make_async_copy(out.at[rows], err_hbm.at[rows, pl.ds(HALF, HALF)], sem.at[b])
         copy.start()
         stores.append(copy)
     for copy in stores:
@@ -409,9 +424,10 @@
             pltpu.VMEM(wide, F32),
             pltpu.VMEM((ROWS, 128), BF16),
             pltpu.VMEM((RANK, COLS), F32),
+            pltpu.VMEM((ROWS, HALF), BF16),
         ),
         in_specs=[anyspace, anyspace, anyspace],
-        out_specs=(vmem, vmem, vmem),
+        out_specs=(vmem, vmem, vmem, vmem),
         scratch_shapes=[
             pltpu.VMEM((2,) + grouped, BF16),
             pltpu.VMEM((RANK, COLS), F32),
@@ -442,9 +458,9 @@
         update_kernel,
         name="update",
         out_shape=(jax.ShapeDtypeStruct(wide, BF16), jax.ShapeDtypeStruct((RANK, COLS), F32)),
-        in_specs=[vmem, vmem, vmem],
+        in_specs=[vmem, vmem, vmem, vmem],
         out_specs=(anyspace, anyspace),
-        scratch_shapes=[pltpu.VMEM(wide, BF16), dma((ROWS // BLOCK + 1,))],
+        scratch_shapes=[pltpu.VMEM((ROWS, HALF), BF16), dma((ROWS // BLOCK + 2,))],
         compiler_params=pltpu.CompilerParams(vmem_limit_bytes=24 * 1024 * 1024),
     )(*(pltpu.with_memory_space_constraint(x, pltpu.VMEM) for x in kept))
     return new_errors[None], basis_t.T

time: 47.3 us -> 46.7 us (0.987)
  Pallas kernels: 46.5 us -> 45.9 us
where the time goes in v6:
time: 46.7 us; the launch traced here: 46.6 us
  Pallas kernels  45.9 us (98%)
  between operations  0.64 us (1%)
    pallas_call x1, Pallas kernels, on_device(): pl.pallas_call(factors_kernel, name='factors', out_shape=(pltpu.VMEM(wide...  44.8 us
    pallas_call x1, Pallas kernels, on_device(): pl.pallas_call(update_kernel, name='update', out_shape=(jax.ShapeDtypeStr...  1.17 us

profile of v6, /device:TPU:1, one launch (start us, length us, event | category | flops | bytes accessed | tf_op | source)
XLA Modules:
  0.0 46.6 jit_solution(5464341431565273999)
XLA Ops:
  0.6 44.8 %factors.1 = (f32[1344,512]{1,0:T(8,128)S(1)}, bf16[1344,128]{1,0:T(8,128)(2,1)S(1)}, f32[32,512]{1,0:T(8,128)S(1)}, bf16[1344,256]{1,0:T(8,128)(2,1)S(1)}) custom-call(bf16[4,336,512]{2,1,0:T(8,128)(2,1)} %bitcast.5, bf16[4,336,512]{2,1,0:T(8,128)(2,1)} %bitcast.6, f32[32,512]{1,0:T(8,128)} %bitcast.7), custom_call_target="tpu_custom_call" | custom-call | tf_op jit(solution)/shard_map/factors/pallas_call | solution.py:420
  45.4 1.2 %update.1 = (bf16[1344,512]{1,0:T(8,128)(2,1)}, f32[32,512]{1,0:T(8,128)}) custom-call(f32[1344,512]{1,0:T(8,128)S(1)} %get-tuple-element.8.merged, bf16[1344,128]{1,0:T(8,128)(2,1)S(1)} %get-tuple-element.9.lhs_ref, f32[32,512]{1,0:T(8,128)S(1)} %get-tuple-element.10.basis_ref, bf16[1344,256]{1,0:T(8,128)(2,1)S(1)} %get-tuple-element.11.done), custom_call_target="tpu_custom_call" | custom-call | tf_op jit(solution)/shard_map/update/pallas_call | solution.py:457
